TPU v7x, 32 devices: a whole 2x2x4 slice. The times are simulated.
32 devices in a mesh: gx: 16 (over z, x, core), gy: 2 (over y).
Axes of the slice: x: 2, y: 2, z: 4, core: 2. Of those that a mesh axis runs over, the one named last changes fastest.
Arguments:
- density: float32 [32, 24, 6912], P('gx', None, 'gy'), may hold values from 0.05 to 1
- gains_a: float32 [8, 24, 24, 24], replicated, may hold values from -6 to 6
- gains_b: float32 [8, 24, 24, 24], replicated, may hold values from -6 to 6
- loss_rates: float32 [24, 24, 24], replicated, may hold values from 0.1 to 1
Outputs:
- evolved: float32 [32, 24, 6912], P('gx', None, 'gy')
All inputs are finite; a program needn't handle non-finite values.
Results may differ from a plain program's by a relative error of at most 0.0001.
Values sent between devices are 32-bit elements; how exact they have to be, the bound alone decides.
No kernel may reach another device: no remote copies, remote signals or barrier semaphores. Data moves between devices by JAX's collectives and lax.ppermute only.
A program may use at most 128 MiB of HBM per device.

v0:
```python
import functools

import jax
import jax.numpy as jnp
import numpy as np
from jax import lax
from jax.experimental import pallas as pl
from jax.experimental.pallas import tpu as pltpu
from jax.sharding import PartitionSpec as P

courant_max = 1.6
collide_step = 0.2
lanes = 128
bf16 = jnp.bfloat16
f32 = jnp.float32
dot = functools.partial(jnp.dot, preferred_element_type=f32)


def passed_along(value, axis, steps):
    count = lax.axis_size(axis)
    pairs = [(source, (source + steps) % count) for source in range(count)]
    return lax.ppermute(value, axis, pairs)


def cosine_table(count):
    freq = np.arange(count)[:, None]
    points = np.arange(count)[None, :]
    scale = np.where(freq == 0, np.sqrt(1.0 / count), np.sqrt(2.0 / count))
    return scale * np.cos(np.pi * (2.0 * points + 1.0) * freq / (2.0 * count))


def two_parts(table):
    high = np.asarray(table, np.float32).astype(bf16)
    return high, (table - high.astype(np.float64)).astype(np.float32).astype(bf16)


def courant_weights(count):
    speeds = np.arange(count) - (count - 1) / 2.0
    a = courant_max * np.abs(speeds) / ((count - 1) / 2.0)
    return np.stack([1.0 - 1.5 * a + 0.5 * a * a, 2.0 * a - a * a, 0.5 * (a * a - a)])


def sign(s, q):
    return -1.0 if ((s >> 1) & (q >> 1)) ^ (s & 1 & q) else 1.0


def block_table(count, q):
    c = cosine_table(count)
    half = count // 2
    return np.kron(c[q >> 1 :: 2, :half], c[q & 1 :: 2, :half])


def point_lanes(count):
    half = count // 2
    block = half * half
    rest = block - lanes
    source = np.full(5 * lanes, -1, np.int32)
    for s in range(4):
        for m in range(block):
            j, l = divmod(m, half)
            y = count - 1 - j if s >> 1 else j
            z = count - 1 - l if s & 1 else l
            if m < lanes:
                source[s * lanes + m] = y * count + z
            else:
                for copy in range(2):
                    source[4 * lanes + copy * 4 * rest + s * rest + m - lanes] = y * count + z
    return source


def mode_lanes(count):
    half = count // 2
    block = half * half
    rest = block - lanes
    source = np.full(6 * lanes, -1, np.int32)
    for q in range(4):
        for m in range(block):
            j, l = divmod(m, half)
            place = (2 * j + (q >> 1)) * count + 2 * l + (q & 1)
            if m < lanes:
                source[q * lanes + m] = place
            else:
                for copy in range(3):
                    source[(4 + q // 2) * lanes + copy * 2 * rest + (q % 2) * rest + m - lanes] = place
    return source


def inverse_tables(count):
    rest = (count // 2) ** 2 - lanes
    out = np.zeros((4, 4 * lanes, 2 * lanes), bf16)
    for q in range(4):
        table = block_table(count, q)
        wide = np.zeros((table.shape[0], 2 * lanes))
        wide[:, :lanes] = table[:, :lanes]
        for s in range(4):
            for copy in range(2):
                at = lanes + copy * 4 * rest + s * rest
                wide[:, at : at + rest] = sign(s, q) * table[:, lanes:]
        high, low = two_parts(wide)
        out[q, :lanes] = high[:lanes]
        out[q, lanes : 2 * lanes] = high[:lanes]
        out[q, 2 * lanes : 3 * lanes] = low[:lanes]
        for copy, part in enumerate((high, high, low)):
            at = 3 * lanes + copy * 2 * rest + (q % 2) * rest
            out[q, at : at + rest] = part[lanes:]
    return out


def forward_tables(count):
    rest = (count // 2) ** 2 - lanes
    out = np.zeros((4, 5 * lanes, 2 * lanes), bf16)
    for q in range(4):
        table = block_table(count, q).T
        wide = np.zeros((table.shape[0], 2 * lanes))
        wide[:, :lanes] = table[:, :lanes]
        for copy in range(3):
            at = lanes + copy * 2 * rest + (q % 2) * rest
            wide[:, at : at + rest] = table[:, lanes:]
        high, low = two_parts(wide)
        out[q, :lanes] = high[:lanes]
        out[q, lanes : 2 * lanes] = high[:lanes]
        out[q, 2 * lanes : 3 * lanes] = low[:lanes]
        for s in range(4):
            for at, part in ((3 * lanes, high), (3 * lanes + 4 * rest, high), (4 * lanes, low)):
                at = at + s * rest
                out[q, at : at + rest] = (sign(s, q) * part[lanes:].astype(np.float32)).astype(bf16)
    return out


def row_tables(count, cells):
    c = cosine_table(count)
    result = []
    for table in (c, c.T):
        high, low = two_parts(np.kron(np.eye(cells), table))
        result.append(np.concatenate([high, high, low], axis=1))
    return np.stack(result)


def split(value):
    high = value.astype(bf16)
    return high, (value - high.astype(f32)).astype(bf16)


def lane_index():
    return lax.broadcasted_iota(jnp.int32, (1, lanes), 1)


def tile(value, at):
    return value[:, at * lanes : (at + 1) * lanes]


def crossed(v0, v1, v2, v3):
    t0, t1, t2, t3 = v0 + v1, v0 - v1, v2 + v3, v2 - v3
    return t0 + t2, t1 + t3, t0 - t2, t1 - t3


def stacked_rows(value):
    high, low = split(value)
    return jnp.concatenate([high, low, high], axis=0)


def forward(value, table_ref, row_table, rest):
    mixed = crossed(*[tile(value, s) for s in range(4)])
    high, low = split(tile(value, 4))
    both = jnp.where(lane_index() < 4 * rest, high.astype(f32), low.astype(f32)).astype(bf16)
    found = []
    for q in range(4):
        q_high, q_low = split(mixed[q])
        found.append(dot(jnp.concatenate([q_high, q_low, q_high, both, high], axis=1), table_ref[q]))
    modes = jnp.concatenate(
        [tile(v, 0) for v in found] + [tile(found[0], 1) + tile(found[1], 1), tile(found[2], 1) + tile(found[3], 1)],
        axis=1,
    )
    return dot(row_table, stacked_rows(modes))


def inverse_plane(modes, table_ref, rest):
    low_lanes = (lane_index() >= 2 * rest) & (lane_index() < 4 * rest)
    both = []
    for pair in range(2):
        value = tile(modes, 4 + pair)
        high = value.astype(bf16).astype(f32)
        both.append(jnp.where(low_lanes, value - high, high).astype(bf16))
    found = []
    for q in range(4):
        high, low = split(tile(modes, q))
        found.append(dot(jnp.concatenate([high, low, high, both[q // 2]], axis=1), table_ref[q]))
    main = crossed(*[tile(v, 0) for v in found])
    last = (tile(found[0], 1) + tile(found[1], 1)) + (tile(found[2], 1) + tile(found[3], 1))
    return jnp.concatenate(list(main) + [last], axis=1)


def collide(field_ref, modes_ref, sum_ref, kernel_ref, inverse_ref, forward_ref, rows_ref, count, rest, terms):
    units, rows, _ = field_ref.shape
    cells = rows // count
    fwd_rows = rows_ref[0]
    inv_rows = rows_ref[1]

    def scaled(u, factor):
        modes = modes_ref[u].reshape(cells, count, 6 * lanes)
        return (modes * factor[None]).reshape(rows, 6 * lanes)

    for u in range(units):
        modes_ref[u] = forward(field_ref[u], forward_ref, fwd_rows, rest)
    for u in range(units):
        plane = inverse_plane(scaled(u, kernel_ref[2 * terms]), inverse_ref, rest)
        sum_ref[u] = -field_ref[u] * dot(inv_rows, stacked_rows(plane))

    def term(p, carry):
        for u in range(units):
            both = jnp.concatenate([scaled(u, kernel_ref[p]), scaled(u, kernel_ref[terms + p])], axis=0)
            plane = inverse_plane(both, inverse_ref, rest)
            pair = jnp.concatenate([stacked_rows(plane[:rows]), stacked_rows(plane[rows:])], axis=1)
            found = dot(inv_rows, pair)
            sum_ref[u] += found[:, : 5 * lanes] * found[:, 5 * lanes :]
        return carry

    lax.fori_loop(0, terms, term, 0)
    for u in range(units):
        field_ref[u] = field_ref[u] + collide_step * sum_ref[u]


def one_hot(source_row, rows):
    index = lax.broadcasted_iota(jnp.int32, (rows, source_row.shape[1]), 0)
    return jnp.where(index == source_row, 1.0, 0.0).astype(bf16)


def moved(value, table):
    high, low = split(value)
    return dot(high, table) + dot(low, table)


def pack_kernel(count, source_ref, a_ref, b_ref, loss_ref, out_ref):
    table = one_hot(source_ref[...], count * count)

    def packed(ref, start, matrices):
        rows = matrices * count
        parts = [ref[pl.ds(start * count * count + k, rows, stride=count), :] for k in range(count)]
        return moved(jnp.concatenate(parts, axis=1), table).reshape(matrices, count, 6 * lanes)

    terms = a_ref.shape[0] // (count * count)
    out_ref[:terms] = packed(a_ref, 0, terms)
    out_ref[terms : 2 * terms] = packed(b_ref, 0, terms)
    out_ref[2 * terms :] = packed(loss_ref, 0, 1)


def cell_order(cells_y):
    return list(range(0, cells_y, 2)) + list(range(1, cells_y, 2))


def first_kernel(
    count, rest, terms, cells_y,
    density_ref, below_ref, above_ref, kernel_ref, inverse_ref, forward_ref, rows_ref, speed_ref, source_ref,
    field_ref, up_ref, down_ref, modes_ref, sum_ref, rim_ref,
):
    cells_x = density_ref.shape[0]
    middle = count // 2
    plane = count * count
    for i in range(2):
        rim_ref[i, :middle] = above_ref[i]
        rim_ref[i, middle:] = below_ref[i]
    positive = lax.broadcasted_iota(jnp.int32, (count, 1), 0) >= middle
    tables = [one_hot(source_ref[k : k + 1], 5 * lanes) for k in range(2)]

    def behind(x):
        return density_ref[x] if x >= 0 else rim_ref[x + 2]

    def ahead(x):
        return density_ref[x] if x < cells_x else rim_ref[x - cells_x]

    for x in range(cells_x):
        w0, w1, w2 = [speed_ref[:, k : k + 1] for k in range(3)]
        near = jnp.where(positive, behind(x - 1), ahead(x + 1))
        far = jnp.where(positive, behind(x - 2), ahead(x + 2))
        moved_on = w0 * density_ref[x] + w1 * near + w2 * far
        pieces = []
        for odd in range(2):
            parts = []
            for y in range(odd, cells_y, 2):
                at = y * plane - odd * (lanes // 2)
                parts.append(moved_on[:, at : at + 5 * lanes])
            pieces.append(moved(jnp.concatenate(parts, axis=0), tables[odd]))
        field_ref[x] = jnp.concatenate(pieces, axis=0)
    collide(field_ref, modes_ref, sum_ref, kernel_ref, inverse_ref, forward_ref, rows_ref, count, rest, terms)
    order = cell_order(cells_y)
    for x in range(cells_x):
        for k in range(2):
            at = order.index(cells_y - 2 + k) * count
            up_ref[x, k] = field_ref[x, at : at + count, 2 * lanes :]
            at = order.index(k) * count
            down_ref[x, k, :, : 2 * lanes] = field_ref[x, at : at + count, : 2 * lanes]
            down_ref[x, k, :, 2 * lanes :] = field_ref[x, at : at + count, 4 * lanes :]


def second_kernel(
    count, rest, terms, cells_y,
    given_ref, below_ref, above_ref, kernel_ref, inverse_ref, forward_ref, rows_ref, speed_ref, source_ref,
    out_ref, field_ref, modes_ref, sum_ref,
):
    cells_x = given_ref.shape[0]
    plane = count * count
    order = cell_order(cells_y)
    backward_last = (lane_index() // (2 * rest)) % 2 == 1
    for x in range(cells_x):

        def cell(y, part):
            if y < 0:
                return below_ref[x, y + 2, :, (part - 2) * lanes : (part - 1) * lanes]
            if y >= cells_y:
                at = part if part < 2 else 2
                return above_ref[x, y - cells_y, :, at * lanes : (at + 1) * lanes]
            at = order.index(y) * count
            return given_ref[x, at : at + count, part * lanes : (part + 1) * lanes]

        for y in range(cells_y):
            at = order.index(y) * count
            for part in range(5):
                w0, w1, w2 = [speed_ref[k : k + 1, part * lanes : (part + 1) * lanes] for k in range(3)]
                if part < 2:
                    near, far = cell(y + 1, part), cell(y + 2, part)
                elif part < 4:
                    near, far = cell(y - 1, part), cell(y - 2, part)
                else:
                    near = jnp.where(backward_last, cell(y - 1, part), cell(y + 1, part))
                    far = jnp.where(backward_last, cell(y - 2, part), cell(y + 2, part))
                field_ref[x, at : at + count, part * lanes : (part + 1) * lanes] = (
                    w0 * cell(y, part) + w1 * near + w2 * far
                )
    collide(field_ref, modes_ref, sum_ref, kernel_ref, inverse_ref, forward_ref, rows_ref, count, rest, terms)
    tables = [one_hot(source_ref[k : k + 1], 5 * lanes) for k in range(2)]
    half = (cells_y // 2) * count
    for x in range(cells_x):
        even = moved(field_ref[x, :half], tables[0])
        odd = moved(field_ref[x, half:], tables[1])
        for k in range(cells_y // 2):
            first = even[k * count : (k + 1) * count]
            second = odd[k * count : (k + 1) * count]
            pair = [tile(first, t) for t in range(4)] + [tile(first, 4) + tile(second, 0)]
            pair += [tile(second, t) for t in range(1, 5)]
            out_ref[x, :, 2 * k * plane : 2 * (k + 1) * plane] = jnp.concatenate(pair, axis=1)


def body(density, gains_a, gains_b, loss_rates):
    cells_x, count, _ = density.shape
    terms = gains_a.shape[0]
    middle = count // 2
    plane = count * count
    cells_y = density.shape[2] // plane
    rest = middle * middle - lanes
    rows = cells_y * count
    points = point_lanes(count)
    natural = np.full((2, 5 * lanes), -1, np.int32)
    for lane in range(4 * lanes + 4 * rest):
        natural[0, points[lane]] = lane
        natural[1, points[lane] + lanes // 2] = lane
    fold = np.where(points >= 0, np.stack([points, points + lanes // 2]), -1).astype(np.int32)
    weights = courant_weights(count)
    lane_speed = np.where(points >= 0, weights[:, points // count], 0.0).astype(np.float32)
    inverse = jnp.asarray(inverse_tables(count))
    forward_table = jnp.asarray(forward_tables(count))
    row_table = jnp.asarray(row_tables(count, cells_y))
    params = pltpu.CompilerParams(vmem_limit_bytes=56 << 20)

    below = passed_along(density[-2:, middle:], "gx", 1)
    above = passed_along(density[:2, :middle], "gx", -1)
    packed = pl.pallas_call(
        functools.partial(pack_kernel, count),
        out_shape=jax.ShapeDtypeStruct((2 * terms + 1, count, 6 * lanes), f32),
        compiler_params=params,
        cost_estimate=pl.CostEstimate(flops=4 << 30, bytes_accessed=8 << 20, transcendentals=0),
        name="pack",
    )(
        jnp.asarray(mode_lanes(count)[None]),
        gains_a.reshape(-1, count),
        gains_b.reshape(-1, count),
        loss_rates.reshape(-1, count),
    )
    field_shape = jax.ShapeDtypeStruct((cells_x, rows, 5 * lanes), f32)
    rim_shape = jax.ShapeDtypeStruct((cells_x, 2, count, 3 * lanes), f32)
    modes_scratch = pltpu.VMEM((cells_x, rows, 6 * lanes), f32)
    points_scratch = pltpu.VMEM((cells_x, rows, 5 * lanes), f32)
    field, up, down = pl.pallas_call(
        functools.partial(first_kernel, count, rest, terms, cells_y),
        out_shape=(field_shape, rim_shape, rim_shape),
        scratch_shapes=[modes_scratch, points_scratch, pltpu.VMEM((2, count, density.shape[2]), f32)],
        compiler_params=params,
        name="first",
    )(
        density, below, above, packed, inverse, forward_table, row_table,
        jnp.asarray(weights.T.astype(np.float32)), jnp.asarray(fold),
    )
    y_below = passed_along(up, "gy", 1)
    y_above = passed_along(down, "gy", -1)
    return pl.pallas_call(
        functools.partial(second_kernel, count, rest, terms, cells_y),
        out_shape=jax.ShapeDtypeStruct(density.shape, f32),
        scratch_shapes=[points_scratch, modes_scratch, points_scratch],
        compiler_params=params,
        name="second",
    )(
        field, y_below, y_above, packed, inverse, forward_table, row_table,
        jnp.asarray(lane_speed), jnp.asarray(natural),
    )


def solution(mesh):
    in_specs = (P("gx", None, "gy"), P(), P(), P())
    out_specs = P("gx", None, "gy")
    return jax.shard_map(body, mesh=mesh, in_specs=in_specs, out_specs=out_specs, check_vma=False)
```

profile of v0, /device:TPU:0, one launch (start us, length us, event | category | flops | bytes accessed | tf_op | source)
XLA Modules:
  0.0 63.5 jit_solution(17915331621507835231)
XLA Ops:
  0.0 1.2 %fusion = (f32[2,12,3456]{2,1,0:T(8,128)S(1)}, f32[2,12,3456]{2,1,0:T(8,128)S(1)}) fusion(f32[2,24,3456]{2,1,0:T(8,128)} %density_ref.1), kind=kLoop, calls=%fused_computation | loop fusion | bytes 1327104 | tf_op jit(solution)/shard_map/slice | solution.py:365
  1.2 5.5 %collective-permute-start.1 = (f32[2,12,3456]{2,1,0:T(8,128)S(1)}, f32[2,12,3456]{2,1,0:T(8,128)S(1)}, u32[]{:S(2)}, u32[]{:S(2)}) collective-permute-start(f32[2,12,3456]{2,1,0:T(8,128)S(1)} %get-tuple-element.11), channel_id=1, source_target_pairs={{0,30},{2,0},{4,2},{6,4},{8,6},{10,8},{12,10},{14,12},{16,14},{18,... | collective-permute-start | bytes 995336 | tf_op jit(solution)/shard_map/ppermute | solution.py:22
  6.7 0.0 collective-permute-start
  6.7 5.5 %pack.1.kernel_ref = f32[17,24,768]{2,1,0:T(8,128)} custom-call(s32[1,768]{1,0:T(1,128)} %constant.19.clone.source_ref, f32[4608,24]{1,0:T(8,128)} %bitcast.3, f32[4608,24]{1,0:T(8,128)} %bitcast.4, f32[576,24]{1,0:T(8,128)} %bitcast.5), custom_call_target="tpu_custom_call" | custom-call | flops 4294967296 | bytes 8388608 | tf_op jit(solution)/shard_map/pack/pallas_call | solution.py:366
  12.2 0.3 collective-permute-done.1.above_ref
  12.5 0.0 copy-start
  12.5 4.6 %collective-permute-done.below_ref = f32[2,12,3456]{2,1,0:T(8,128)S(1)} collective-permute-done((f32[2,12,3456]{2,1,0:T(8,128)S(1)}, f32[2,12,3456]{2,1,0:T(8,128)S(1)}, u32[]{:S(2)}, u32[]{:S(2)}) %collective-permute-start) | collective-permute-done | bytes 331808 | tf_op jit(solution)/shard_map/ppermute | solution.py:22
  17.1 0.0 copy-done
  17.1 0.0 copy-start.1
  17.1 0.8 %copy-done.1 = f32[2,12,3456]{2,1,0:T(8,128)} copy-done((f32[2,12,3456]{2,1,0:T(8,128)}, f32[2,12,3456]{2,1,0:T(8,128)S(1)}, u32[]{:S(2)}) %copy-start.1) | copy-done | bytes 331800
  17.9 19.1 %first.1 = (f32[2,144,640]{2,1,0:T(8,128)}, f32[2,2,24,384]{3,2,1,0:T(8,128)}, f32[2,2,24,384]{3,2,1,0:T(8,128)}) custom-call(f32[2,24,3456]{2,1,0:T(8,128)} %density_ref.1, f32[2,12,3456]{2,1,0:T(8,128)} %copy-done.1, f32[2,12,3456]{2,1,0:T(8,128)} %copy-done, f32[17,24,768]{2,1,0:T(8,128)} %pack.1.kernel_ref, ...), custom_call_target="tpu_custom_call" | custom-call | tf_op jit(solution)/shard_map/first/pallas_call | solution.py:382
  37.0 1.5 %collective-permute-start.2 = (f32[2,2,24,384]{3,2,1,0:T(8,128)}, f32[2,2,24,384]{3,2,1,0:T(8,128)S(1)}, u32[]{:S(2)}, u32[]{:S(2)}) collective-permute-start(f32[2,2,24,384]{3,2,1,0:T(8,128)} %get-tuple-element.9), channel_id=1, source_target_pairs={{0,1},{1,0},{2,3},{3,2},{4,5},{5,4},{6,7},{7,6},{8,9},{9,8},{10,11... | collective-permute-start | bytes 442376 | tf_op jit(solution)/shard_map/ppermute | solution.py:22
  38.5 0.5 collective-permute-start.3
  39.0 3.3 %collective-permute-done.2.below_ref = f32[2,2,24,384]{3,2,1,0:T(8,128)S(1)} collective-permute-done((f32[2,2,24,384]{3,2,1,0:T(8,128)}, f32[2,2,24,384]{3,2,1,0:T(8,128)S(1)}, u32[]{:S(2)}, u32[]{:S(2)}) %collective-permute-start.2) | collective-permute-done | bytes 147488 | tf_op jit(solution)/shard_map/ppermute | solution.py:22
  42.4 0.0 copy-start.2
  42.4 1.6 %collective-permute-done.3.above_ref = f32[2,2,24,384]{3,2,1,0:T(8,128)S(1)} collective-permute-done((f32[2,2,24,384]{3,2,1,0:T(8,128)}, f32[2,2,24,384]{3,2,1,0:T(8,128)S(1)}, u32[]{:S(2)}, u32[]{:S(2)}) %collective-permute-start.3) | collective-permute-done | bytes 147488 | tf_op jit(solution)/shard_map/ppermute | solution.py:22
  43.9 0.0 copy-start.3
  43.9 0.0 copy-done.2
  43.9 0.6 %copy-done.3 = f32[2,2,24,384]{3,2,1,0:T(8,128)} copy-done((f32[2,2,24,384]{3,2,1,0:T(8,128)}, f32[2,2,24,384]{3,2,1,0:T(8,128)S(1)}, u32[]{:S(2)}) %copy-start.3) | copy-done | bytes 147480
  44.6 18.9 %second.1 = f32[2,24,3456]{2,1,0:T(8,128)} custom-call(f32[2,144,640]{2,1,0:T(8,128)} %get-tuple-element.8.given_ref, f32[2,2,24,384]{3,2,1,0:T(8,128)} %copy-done.2, f32[2,2,24,384]{3,2,1,0:T(8,128)} %copy-done.3, f32[17,24,768]{2,1,0:T(8,128)} %pack.1.kernel_ref, bf16[4,512,256]{2,1,0:T(8,128)(2,1)} %constant.16.clone.inverse_ref, ...), custom_call_target="tpu_custom_call" | custom-call | tf_op jit(solution)/shard_map/second/pallas_call | solution.py:394
Async XLA Ops:
  1.2 11.3 %collective-permute-start.1 = (f32[2,12,3456]{2,1,0:T(8,128)S(1)}, f32[2,12,3456]{2,1,0:T(8,128)S(1)}, u32[]{:S(2)}, u32[]{:S(2)}) collective-permute-start(f32[2,12,3456]{2,1,0:T(8,128)S(1)} %get-tuple-element.11), channel_id=1, source_target_pairs={{0,30},{2,0},{4,2},{6,4},{8,6},{10,8},{12,10},{14,12},{16,14},{18,... | collective-permute-start | bytes 995336 | tf_op jit(solution)/shard_map/ppermute | solution.py:22
  6.7 10.4 %collective-permute-start = (f32[2,12,3456]{2,1,0:T(8,128)S(1)}, f32[2,12,3456]{2,1,0:T(8,128)S(1)}, u32[]{:S(2)}, u32[]{:S(2)}) collective-permute-start(f32[2,12,3456]{2,1,0:T(8,128)S(1)} %get-tuple-element.12), channel_id=1, source_target_pairs={{0,2},{2,4},{4,6},{6,8},{8,10},{10,12},{12,14},{14,16},{16,18},{18... | collective-permute-start | bytes 995336 | tf_op jit(solution)/shard_map/ppermute | solution.py:22
  12.5 4.6 %copy-start = (f32[2,12,3456]{2,1,0:T(8,128)}, f32[2,12,3456]{2,1,0:T(8,128)S(1)}, u32[]{:S(2)}) copy-start(f32[2,12,3456]{2,1,0:T(8,128)S(1)} %collective-permute-done.1.above_ref) | copy-start | bytes 995332
  17.1 0.8 %copy-start.1 = (f32[2,12,3456]{2,1,0:T(8,128)}, f32[2,12,3456]{2,1,0:T(8,128)S(1)}, u32[]{:S(2)}) copy-start(f32[2,12,3456]{2,1,0:T(8,128)S(1)} %collective-permute-done.below_ref) | copy-start | bytes 995332
  37.0 5.4 %collective-permute-start.2 = (f32[2,2,24,384]{3,2,1,0:T(8,128)}, f32[2,2,24,384]{3,2,1,0:T(8,128)S(1)}, u32[]{:S(2)}, u32[]{:S(2)}) collective-permute-start(f32[2,2,24,384]{3,2,1,0:T(8,128)} %get-tuple-element.9), channel_id=1, source_target_pairs={{0,1},{1,0},{2,3},{3,2},{4,5},{5,4},{6,7},{7,6},{8,9},{9,8},{10,11... | collective-permute-start | bytes 442376 | tf_op jit(solution)/shard_map/ppermute | solution.py:22
  38.5 5.4 %collective-permute-start.3 = (f32[2,2,24,384]{3,2,1,0:T(8,128)}, f32[2,2,24,384]{3,2,1,0:T(8,128)S(1)}, u32[]{:S(2)}, u32[]{:S(2)}) collective-permute-start(f32[2,2,24,384]{3,2,1,0:T(8,128)} %get-tuple-element.10), channel_id=1, source_target_pairs={{0,1},{1,0},{2,3},{3,2},{4,5},{5,4},{6,7},{7,6},{8,9},{9,8},{10,11... | collective-permute-start | bytes 442376 | tf_op jit(solution)/shard_map/ppermute | solution.py:22
  42.4 1.6 %copy-start.2 = (f32[2,2,24,384]{3,2,1,0:T(8,128)}, f32[2,2,24,384]{3,2,1,0:T(8,128)S(1)}, u32[]{:S(2)}) copy-start(f32[2,2,24,384]{3,2,1,0:T(8,128)S(1)} %collective-permute-done.2.below_ref) | copy-start | bytes 442372
  43.9 0.7 %copy-start.3 = (f32[2,2,24,384]{3,2,1,0:T(8,128)}, f32[2,2,24,384]{3,2,1,0:T(8,128)S(1)}, u32[]{:S(2)}) copy-start(f32[2,2,24,384]{3,2,1,0:T(8,128)S(1)} %collective-permute-done.3.above_ref) | copy-start | bytes 442372
where the time goes:
time: 63.6 us; the launch traced here: 63.5 us
  Pallas kernels  43.5 us (68%)
  waiting for transfers between devices  9.79 us (15%)
  starting transfers between devices  7.53 us (12%)
  local copies, waits for them, and re-layouts  2.62 us (4%)
    pallas_call x1, Pallas kernels, body(): pl.pallas_call(functools.partial(first_kernel, count, rest, terms, cells_...  19.1 us
    pallas_call x1, Pallas kernels, body(): pl.pallas_call(functools.partial(second_kernel, count, rest, terms, cells...  18.9 us
    ppermute x4, waiting for transfers between devices, passed_along(): return lax.ppermute(value, axis, pairs)  9.79 us
    ppermute x4, starting transfers between devices, passed_along(): return lax.ppermute(value, axis, pairs)  7.53 us
    pallas_call x1, Pallas kernels, body(): pl.pallas_call(functools.partial(pack_kernel, count), out_shape=jax.Shape...  5.54 us
    unnamed x8, local copies, waits for them, and re-layouts  1.42 us
  transfers between devices with their start and end apart: 4, of which 4 were waited for; matrix products, arithmetic and copies ran while one was open for 0% of the time, Pallas kernels for 9%

commit v1 on v0

v1 whole, which is shorter than its diff:
```python
import functools

import jax
import jax.numpy as jnp
import numpy as np
from jax import lax
from jax.experimental import pallas as pl
from jax.experimental.pallas import tpu as pltpu
from jax.sharding import PartitionSpec as P

courant_max = 1.6
collide_step = 0.2
lanes = 128
bf16 = jnp.bfloat16
f32 = jnp.float32
dot = functools.partial(jnp.dot, preferred_element_type=f32)


def passed_along(value, axis, steps):
    count = lax.axis_size(axis)
    pairs = [(source, (source + steps) % count) for source in range(count)]
    return lax.ppermute(value, axis, pairs)


def cosine_table(count):
    freq = np.arange(count)[:, None]
    points = np.arange(count)[None, :]
    scale = np.where(freq == 0, np.sqrt(1.0 / count), np.sqrt(2.0 / count))
    return scale * np.cos(np.pi * (2.0 * points + 1.0) * freq / (2.0 * count))


def two_parts(table):
    high = np.asarray(table, np.float32).astype(bf16)
    return high, (table - high.astype(np.float64)).astype(np.float32).astype(bf16)


def courant_weights(count):
    speeds = np.arange(count) - (count - 1) / 2.0
    a = courant_max * np.abs(speeds) / ((count - 1) / 2.0)
    return np.stack([1.0 - 1.5 * a + 0.5 * a * a, 2.0 * a - a * a, 0.5 * (a * a - a)])


def sign(s, q):
    return -1.0 if ((s >> 1) & (q >> 1)) ^ (s & 1 & q) else 1.0


def block_table(count, q):
    c = cosine_table(count)
    half = count // 2
    return np.kron(c[q >> 1 :: 2, :half], c[q & 1 :: 2, :half])


def point_lanes(count):
    half = count // 2
    block = half * half
    rest = block - lanes
    source = np.full(5 * lanes, -1, np.int32)
    for s in range(4):
        for m in range(block):
            j, l = divmod(m, half)
            y = count - 1 - j if s >> 1 else j
            z = count - 1 - l if s & 1 else l
            if m < lanes:
                source[s * lanes + m] = y * count + z
            else:
                for copy in range(2):
                    source[4 * lanes + copy * 4 * rest + s * rest + m - lanes] = y * count + z
    return source


def mode_lanes(count):
    half = count // 2
    block = half * half
    rest = block - lanes
    source = np.full(6 * lanes, -1, np.int32)
    for q in range(4):
        for m in range(block):
            j, l = divmod(m, half)
            place = (2 * j + (q >> 1)) * count + 2 * l + (q & 1)
            if m < lanes:
                source[q * lanes + m] = place
            else:
                for copy in range(3):
                    source[(4 + q // 2) * lanes + copy * 2 * rest + (q % 2) * rest + m - lanes] = place
    return source


def inverse_tables(count):
    rest = (count // 2) ** 2 - lanes
    out = np.zeros((4, 4 * lanes, 2 * lanes), bf16)
    for q in range(4):
        table = block_table(count, q)
        wide = np.zeros((table.shape[0], 2 * lanes))
        wide[:, :lanes] = table[:, :lanes]
        for s in range(4):
            for copy in range(2):
                at = lanes + copy * 4 * rest + s * rest
                wide[:, at : at + rest] = sign(s, q) * table[:, lanes:]
        high, low = two_parts(wide)
        out[q, :lanes] = high[:lanes]
        out[q, lanes : 2 * lanes] = high[:lanes]
        out[q, 2 * lanes : 3 * lanes] = low[:lanes]
        for copy, part in enumerate((high, high, low)):
            at = 3 * lanes + copy * 2 * rest + (q % 2) * rest
            out[q, at : at + rest] = part[lanes:]
    return out


def forward_tables(count):
    rest = (count // 2) ** 2 - lanes
    out = np.zeros((4, 5 * lanes, 2 * lanes), bf16)
    for q in range(4):
        table = block_table(count, q).T
        wide = np.zeros((table.shape[0], 2 * lanes))
        wide[:, :lanes] = table[:, :lanes]
        for copy in range(3):
            at = lanes + copy * 2 * rest + (q % 2) * rest
            wide[:, at : at + rest] = table[:, lanes:]
        high, low = two_parts(wide)
        out[q, :lanes] = high[:lanes]
        out[q, lanes : 2 * lanes] = high[:lanes]
        out[q, 2 * lanes : 3 * lanes] = low[:lanes]
        for s in range(4):
            for at, part in ((3 * lanes, high), (3 * lanes + 4 * rest, high), (4 * lanes, low)):
                at = at + s * rest
                out[q, at : at + rest] = (sign(s, q) * part[lanes:].astype(np.float32)).astype(bf16)
    return out


def row_groups(rows):
    middle = rows // 2
    return ((0, middle, 0, -(-middle // 16) * 16), (middle, rows, middle // 16 * 16, rows))


def row_tables(count, cells):
    c = cosine_table(count)
    result = []
    for table in (c, c.T):
        whole = np.kron(np.eye(cells), table)
        groups = []
        for first, last, low, high in row_groups(cells * count):
            coarse, fine = two_parts(whole[first:last, low:high])
            groups.append(np.concatenate([coarse, coarse, fine], axis=1))
        result.append(np.stack(groups))
    return np.stack(result)


def split(value):
    high = value.astype(bf16)
    return high, (value - high.astype(f32)).astype(bf16)


def lane_index():
    return lax.broadcasted_iota(jnp.int32, (1, lanes), 1)


def tile(value, at):
    return value[:, at * lanes : (at + 1) * lanes]


def crossed(v0, v1, v2, v3):
    t0, t1, t2, t3 = v0 + v1, v0 - v1, v2 + v3, v2 - v3
    return t0 + t2, t1 + t3, t0 - t2, t1 - t3


def along_rows(values, tables, rows):
    parts = [split(value) for value in values]
    found = []
    for g, (_, _, first, last) in enumerate(row_groups(rows)):
        pieces = [
            jnp.concatenate([high[first:last], low[first:last], high[first:last]], axis=0) for high, low in parts
        ]
        found.append(dot(tables[g], jnp.concatenate(pieces, axis=1)))
    return found


def forward(value, table_ref, rest):
    mixed = crossed(*[tile(value, s) for s in range(4)])
    high, low = split(tile(value, 4))
    both = jnp.where(lane_index() < 4 * rest, high.astype(f32), low.astype(f32)).astype(bf16)
    found = []
    for q in range(4):
        q_high, q_low = split(mixed[q])
        found.append(dot(jnp.concatenate([q_high, q_low, q_high, both, high], axis=1), table_ref[q]))
    return jnp.concatenate(
        [tile(v, 0) for v in found] + [tile(found[0], 1) + tile(found[1], 1), tile(found[2], 1) + tile(found[3], 1)],
        axis=1,
    )


def inverse_plane(modes, table_ref, rest):
    low_lanes = (lane_index() >= 2 * rest) & (lane_index() < 4 * rest)
    both = []
    for pair in range(2):
        value = tile(modes, 4 + pair)
        high = value.astype(bf16).astype(f32)
        both.append(jnp.where(low_lanes, value - high, high).astype(bf16))
    found = []
    for q in range(4):
        high, low = split(tile(modes, q))
        found.append(dot(jnp.concatenate([high, low, high, both[q // 2]], axis=1), table_ref[q]))
    main = crossed(*[tile(v, 0) for v in found])
    last = (tile(found[0], 1) + tile(found[1], 1)) + (tile(found[2], 1) + tile(found[3], 1))
    return jnp.concatenate(list(main) + [last], axis=1)


def collide(field_ref, modes_ref, sum_ref, kernel_ref, loss_ref, inverse_ref, forward_ref, rows_ref, count, rest):
    rows = field_ref.shape[0]
    cells = rows // count
    terms = kernel_ref.shape[0]
    together = 2 if terms % 2 == 0 else 1
    wide = 5 * lanes
    groups = [(first, last) for first, last, _, _ in row_groups(rows)]

    def scaled(factor):
        modes = modes_ref[...].reshape(cells, count, 6 * lanes)
        return (modes * factor[None]).reshape(rows, 6 * lanes)

    found = along_rows([forward(field_ref[...], forward_ref, rest)], rows_ref.at[0], rows)
    for (first, last), part in zip(groups, found):
        modes_ref[first:last] = part
    plane = inverse_plane(scaled(loss_ref[...]), inverse_ref, rest)
    found = along_rows([plane], rows_ref.at[1], rows)
    for (first, last), part in zip(groups, found):
        sum_ref[first:last] = -field_ref[first:last] * part

    def term(step, carry):
        factors = [kernel_ref[together * step + k, side] for k in range(together) for side in range(2)]
        plane = inverse_plane(jnp.concatenate([scaled(f) for f in factors], axis=0), inverse_ref, rest)
        planes = [plane[k * rows : (k + 1) * rows] for k in range(2 * together)]
        for (first, last), part in zip(groups, along_rows(planes, rows_ref.at[1], rows)):
            total = sum_ref[first:last]
            for k in range(together):
                at = 2 * k * wide
                total = total + part[:, at : at + wide] * part[:, at + wide : at + 2 * wide]
            sum_ref[first:last] = total
        return carry

    lax.fori_loop(0, terms // together, term, 0)
    field_ref[...] = field_ref[...] + collide_step * sum_ref[...]


def one_hot(source_row, rows):
    index = lax.broadcasted_iota(jnp.int32, (rows, source_row.shape[1]), 0)
    return jnp.where(index == source_row, 1.0, 0.0).astype(bf16)


def moved(value, table):
    high, low = split(value)
    return dot(high, table) + dot(low, table)


def pack_kernel(count, source_ref, a_ref, b_ref, loss_ref, out_ref, loss_out_ref, table_ref):
    @pl.when(pl.program_id(0) == 0)
    def _():
        table_ref[...] = one_hot(source_ref[...], count * count)

    def rows_of(ref):
        rows = ref.shape[0] // count
        return jnp.concatenate([ref[pl.ds(k, rows, stride=count), :] for k in range(count)], axis=1)

    terms = out_ref.shape[0]
    both = jnp.concatenate([rows_of(a_ref), rows_of(b_ref)], axis=0)
    both = moved(both, table_ref[...]).reshape(2, terms, count, 6 * lanes)
    for side in range(2):
        out_ref[:, side] = both[side]

    @pl.when(pl.program_id(0) == 0)
    def _():
        loss_out_ref[...] = moved(rows_of(loss_ref), table_ref[...])


class Half:
    def __init__(self, which, cells_x, cells_y, plane):
        first, last = which * cells_y // 2, (which + 1) * cells_y // 2
        self.cells = range(first, last)
        self.start = first * plane // lanes * lanes
        self.stop = -(-last * plane // lanes) * lanes
        self.shifts = [[y for y in self.cells if y * plane % lanes == shift] for shift in (0, lanes // 2)]
        self.order = [(x, y) for shift in self.shifts for x in range(cells_x) for y in shift]

    def rows(self, x, y, count):
        at = self.order.index((x, y)) * count
        return slice(at, at + count)

    def window(self, y, plane):
        return y * plane // lanes * lanes - self.start


def first_kernel(count, rest, halves, which, *refs):
    density_ref, below_ref, above_ref = refs[:3]
    refs = refs[3:]
    if which:
        earlier, refs = refs[:2], refs[2:]
    kernel_ref, loss_ref, inverse_ref, forward_ref, rows_ref, speed_ref, source_ref = refs[:7]
    out_ref, rim_out_ref, field_ref, modes_ref, sum_ref, rim_ref = refs[7:]
    half = halves[which]
    cells_x = density_ref.shape[0]
    middle = count // 2
    plane = count * count
    known = half.stop - half.start - below_ref.shape[2]
    for i in range(2):
        rim_ref[i, :middle, known:] = above_ref[i]
        rim_ref[i, middle:, known:] = below_ref[i]
        if known:
            rim_ref[i, :middle, :known] = earlier[1][i]
            rim_ref[i, middle:, :known] = earlier[0][i]
    positive = lax.broadcasted_iota(jnp.int32, (count, 1), 0) >= middle
    tables = [one_hot(source_ref[k : k + 1], 5 * lanes) for k in range(2)]

    def own(x):
        return density_ref[x, :, half.start : half.stop]

    def behind(x):
        return own(x) if x >= 0 else rim_ref[x + 2]

    def ahead(x):
        return own(x) if x < cells_x else rim_ref[x - cells_x]

    w0, w1, w2 = [speed_ref[:, k : k + 1] for k in range(3)]
    moved_on = []
    for x in range(cells_x):
        near = jnp.where(positive, behind(x - 1), ahead(x + 1))
        far = jnp.where(positive, behind(x - 2), ahead(x + 2))
        moved_on.append(w0 * own(x) + w1 * near + w2 * far)
    at = 0
    for k, shift in enumerate(half.shifts):
        parts = []
        for x in range(cells_x):
            for y in shift:
                window = half.window(y, plane)
                parts.append(moved_on[x][:, window : window + 5 * lanes])
        size = len(parts) * count
        field_ref[at : at + size] = moved(jnp.concatenate(parts, axis=0), tables[k])
        at += size
    collide(field_ref, modes_ref, sum_ref, kernel_ref, loss_ref, inverse_ref, forward_ref, rows_ref, count, rest)
    out_ref[...] = field_ref[...]
    for x in range(cells_x):
        for k in range(2):
            if which:
                rim_out_ref[x, k] = field_ref[half.rows(x, half.cells[k - 2], count), 2 * lanes :]
            else:
                at = half.rows(x, half.cells[k], count)
                rim_out_ref[x, k, :, : 2 * lanes] = field_ref[at, : 2 * lanes]
                rim_out_ref[x, k, :, 2 * lanes :] = field_ref[at, 4 * lanes :]


def second_kernel(count, rest, halves, which, *refs):
    given = refs[:2]
    rim_ref, kernel_ref, loss_ref, inverse_ref, forward_ref, rows_ref, speed_ref, source_ref = refs[2:10]
    refs = refs[10:]
    if not which:
        upper_ref, refs = refs[0], refs[1:]
    out_ref, field_ref, modes_ref, sum_ref = refs
    half = halves[which]
    cells_x = rim_ref.shape[0]
    cells_y = halves[1].cells[-1] + 1
    plane = count * count
    backward_last = (lane_index() // (2 * rest)) % 2 == 1

    def cell(x, y, part):
        if y < 0:
            return rim_ref[x, y + 2, :, (part - 2) * lanes : (part - 1) * lanes]
        if y >= cells_y:
            at = part if part < 2 else 2
            return rim_ref[x, y - cells_y, :, at * lanes : (at + 1) * lanes]
        place = 0 if y in halves[0].cells else 1
        return given[place][halves[place].rows(x, y, count), part * lanes : (part + 1) * lanes]

    for x, y in half.order:
        for part in range(5):
            w0, w1, w2 = [speed_ref[k : k + 1, part * lanes : (part + 1) * lanes] for k in range(3)]
            if part < 2:
                near, far = cell(x, y + 1, part), cell(x, y + 2, part)
            elif part < 4:
                near, far = cell(x, y - 1, part), cell(x, y - 2, part)
            else:
                near = jnp.where(backward_last, cell(x, y - 1, part), cell(x, y + 1, part))
                far = jnp.where(backward_last, cell(x, y - 2, part), cell(x, y + 2, part))
            field_ref[half.rows(x, y, count), part * lanes : (part + 1) * lanes] = (
                w0 * cell(x, y, part) + w1 * near + w2 * far
            )
    collide(field_ref, modes_ref, sum_ref, kernel_ref, loss_ref, inverse_ref, forward_ref, rows_ref, count, rest)
    at = 0
    pieces = {}
    for k, shift in enumerate(half.shifts):
        cells = [(x, y) for x in range(cells_x) for y in shift]
        size = len(cells) * count
        natural = moved(field_ref[at : at + size], one_hot(source_ref[k : k + 1], 5 * lanes))
        at += size
        for i, place in enumerate(cells):
            pieces[place] = natural[i * count : (i + 1) * count]
    for x in range(cells_x):
        filled = {}
        for y in half.cells:
            window = half.window(y, plane) // lanes
            for t in range(5):
                value = tile(pieces[x, y], t)
                filled[window + t] = filled[window + t] + value if window + t in filled else value
        shared = 0
        if not which:
            shared = halves[1].start // lanes
            for t in range(shared, halves[1].stop // lanes):
                value = upper_ref[x, :, (t - shared) * lanes : (t - shared + 1) * lanes]
                filled[t] = filled[t] + value if t in filled else value
        for t, value in filled.items():
            out_ref[x, :, t * lanes : (t + 1) * lanes] = value


def body(density, gains_a, gains_b, loss_rates):
    cells_x, count, width = density.shape
    terms = gains_a.shape[0]
    middle = count // 2
    plane = count * count
    cells_y = width // plane
    rest = middle * middle - lanes
    halves = [Half(which, cells_x, cells_y, plane) for which in range(2)]
    rows = len(halves[0].order) * count
    points = point_lanes(count)
    natural = np.full((2, 5 * lanes), -1, np.int32)
    for lane in range(4 * lanes + 4 * rest):
        natural[0, points[lane]] = lane
        natural[1, points[lane] + lanes // 2] = lane
    fold = np.where(points >= 0, np.stack([points, points + lanes // 2]), -1).astype(np.int32)
    weights = courant_weights(count)
    lane_speed = np.where(points >= 0, weights[:, points // count], 0.0).astype(np.float32)
    tables = [jnp.asarray(t) for t in (inverse_tables(count), forward_tables(count), row_tables(count, rows // count))]
    row_speed = jnp.asarray(weights.T.astype(np.float32))
    params = pltpu.CompilerParams(vmem_limit_bytes=56 << 20)
    cost = pl.CostEstimate(flops=10 << 30, bytes_accessed=4 << 20, transcendentals=0)
    whole = pl.BlockSpec(memory_space=pltpu.VMEM)

    cut = halves[0].stop
    rims = []
    for first, last in ((0, cut), (cut, width)):
        rims.append(
            (
                passed_along(density[-2:, middle:, first:last], "gx", 1),
                passed_along(density[:2, :middle, first:last], "gx", -1),
            )
        )
    steps = 4 if terms % 4 == 0 else 1
    taken = terms // steps
    gain_spec = pl.BlockSpec((taken * plane, count), lambda i: (i, 0))
    packed, packed_loss = pl.pallas_call(
        functools.partial(pack_kernel, count),
        grid=(steps,),
        in_specs=[
            pl.BlockSpec((1, 6 * lanes), lambda i: (0, 0)),
            gain_spec,
            gain_spec,
            pl.BlockSpec((plane, count), lambda i: (0, 0)),
        ],
        out_specs=[
            pl.BlockSpec((taken, 2, count, 6 * lanes), lambda i: (i, 0, 0, 0)),
            pl.BlockSpec((count, 6 * lanes), lambda i: (0, 0)),
        ],
        out_shape=(
            jax.ShapeDtypeStruct((terms, 2, count, 6 * lanes), f32),
            jax.ShapeDtypeStruct((count, 6 * lanes), f32),
        ),
        scratch_shapes=[pltpu.VMEM((plane, 6 * lanes), bf16)],
        compiler_params=params,
        cost_estimate=pl.CostEstimate(flops=4 << 30, bytes_accessed=8 << 20, transcendentals=0),
        name="pack",
    )(
        jnp.asarray(mode_lanes(count)[None]),
        gains_a.reshape(-1, count),
        gains_b.reshape(-1, count),
        loss_rates.reshape(-1, count),
    )
    field_shape = jax.ShapeDtypeStruct((rows, 5 * lanes), f32)
    rim_shape = jax.ShapeDtypeStruct((cells_x, 2, count, 3 * lanes), f32)
    scratch = [pltpu.VMEM((rows, k * lanes), f32) for k in (5, 6, 5)]
    fields = []
    y_rims = []
    for which, half in enumerate(halves):
        known = half.stop - half.start - rims[which][0].shape[2]
        edge = pl.BlockSpec((2, middle, max(known, 1)), lambda i, at=halves[1].start // max(known, 1): (0, 0, at))
        field, rim = pl.pallas_call(
            functools.partial(first_kernel, count, rest, halves, which),
            grid=(1,) if which else (),
            in_specs=[whole] * 3 + [edge] * (2 * which) + [whole] * 7,
            out_shape=(field_shape, rim_shape),
            scratch_shapes=scratch + [pltpu.VMEM((2, count, half.stop - half.start), f32)],
            compiler_params=params,
            cost_estimate=cost,
            name=f"first_{which}",
        )(
            density, *rims[which], *(rims[0] if which else ()), packed, packed_loss, *tables, row_speed,
            jnp.asarray(fold),
        )
        fields.append(field)
        y_rims.append(passed_along(rim, "gy", 1 if which else -1))
    result = ()
    for which in (1, 0):
        shape = density.shape if not which else (cells_x, count, halves[1].stop - halves[1].start)
        result = (
            pl.pallas_call(
                functools.partial(second_kernel, count, rest, halves, which),
                out_shape=jax.ShapeDtypeStruct(shape, f32),
                scratch_shapes=scratch,
                compiler_params=params,
                cost_estimate=cost,
                name=f"second_{which}",
            )(
                *fields, y_rims[1 - which], packed, packed_loss, *tables, jnp.asarray(lane_speed),
                jnp.asarray(natural), *result,
            ),
        )
    return result[0]


def solution(mesh):
    in_specs = (P("gx", None, "gy"), P(), P(), P())
    out_specs = P("gx", None, "gy")
    return jax.shard_map(body, mesh=mesh, in_specs=in_specs, out_specs=out_specs, check_vma=False)
```

time: 63.6 us -> 66.1 us (1.039)
  waiting for transfers between devices: 9.79 us -> 1.89 us
  starting transfers between devices: 7.53 us -> 12 us
  Pallas kernels: 43.5 us -> 46.4 us
  local copies, waits for them, and re-layouts: 2.62 us -> 5.51 us
    ppermute x4 -> x6, waiting for transfers between devices: 9.79 us -> 1.89 us  [passed_along(): return lax.ppermute(value, axis, pairs)]
    ppermute x4 -> x6, starting transfers between devices: 7.53 us -> 12 us  [passed_along(): return lax.ppermute(value, axis, pairs)]
    pallas_call x3 -> x5, Pallas kernels: 43.5 us -> 46.4 us  [the longest x2 20.3 us: body(): pl.pallas_call(functools.partial(first_kernel, count, rest, halves, which...]
    unnamed x8 -> x12, local copies, waits for them, and re-layouts: 1.42 us -> 3.37 us
    slice x1 -> x2, local copies, waits for them, and re-layouts: 1.21 us -> 2.15 us  [body(): density[:2, :middle, first:last]]
  transfers between devices with their start and end apart: 4 -> 6, of which waited for: 4 -> 1; matrix products, arithmetic and copies ran while one was open for 0% -> 2% of each run, Pallas kernels for 9% -> 55%
where the time goes in v1:
time: 66.1 us; the launch traced here: 65.8 us
  Pallas kernels  46.4 us (70%)
  starting transfers between devices  12 us (18%)
  local copies, waits for them, and re-layouts  5.51 us (8%)
  waiting for transfers between devices  1.89 us (3%)
    pallas_call x2, Pallas kernels, body(): pl.pallas_call(functools.partial(first_kernel, count, rest, halves, which...  20.3 us
    pallas_call x2, Pallas kernels, body(): pl.pallas_call(functools.partial(second_kernel, count, rest, halves, whic...  19.9 us
    ppermute x6, starting transfers between devices, passed_along(): return lax.ppermute(value, axis, pairs)  12 us
    pallas_call x1, Pallas kernels, body(): pl.pallas_call(functools.partial(pack_kernel, count), grid=(steps,), in_s...  6.25 us
    unnamed x12, local copies, waits for them, and re-layouts  3.37 us
    slice x2, local copies, waits for them, and re-layouts, body(): density[:2, :middle, first:last]  2.15 us
    ppermute x6, waiting for transfers between devices, passed_along(): return lax.ppermute(value, axis, pairs)  1.89 us
  transfers between devices with their start and end apart: 6, of which 1 were waited for; matrix products, arithmetic and copies ran while one was open for 2% of the time, Pallas kernels for 55%

profile of v1, /device:TPU:0, one launch (start us, length us, event | category | flops | bytes accessed | tf_op | source)
XLA Modules:
  0.0 65.8 jit_solution(17604761835961128780)
XLA Ops:
  0.0 1.1 %fusion = (f32[2,12,1664]{2,1,0:T(8,128)S(1)}, f32[2,12,1664]{2,1,0:T(8,128)S(1)}) fusion(f32[2,24,3456]{2,1,0:T(8,128)} %refs_0_.3), kind=kLoop, calls=%fused_computation | loop fusion | bytes 638976 | tf_op jit(solution)/shard_map/slice | solution.py:439
  1.1 5.5 %collective-permute-start.3 = (f32[2,12,1664]{2,1,0:T(8,128)S(1)}, f32[2,12,1664]{2,1,0:T(8,128)S(1)}, u32[]{:S(2)}, u32[]{:S(2)}) collective-permute-start(f32[2,12,1664]{2,1,0:T(8,128)S(1)} %get-tuple-element.17), channel_id=1, source_target_pairs={{0,30},{2,0},{4,2},{6,4},{8,6},{10,8},{12,10},{14,12},{16,14},{18,... | collective-permute-start | bytes 479240 | tf_op jit(solution)/shard_map/ppermute | solution.py:22
  6.6 0.0 collective-permute-start.2
  6.6 1.1 %fusion.1 = (f32[2,12,1792]{2,1,0:T(8,128)S(1)}, f32[2,12,1792]{2,1,0:T(8,128)S(1)}) fusion(f32[2,24,3456]{2,1,0:T(8,128)} %refs_0_.3), kind=kLoop, calls=%fused_computation.1 | loop fusion | bytes 688128 | tf_op jit(solution)/shard_map/slice | solution.py:439
  7.7 4.5 %collective-permute-start.1 = (f32[2,12,1792]{2,1,0:T(8,128)S(1)}, f32[2,12,1792]{2,1,0:T(8,128)S(1)}, u32[]{:S(2)}, u32[]{:S(2)}) collective-permute-start(f32[2,12,1792]{2,1,0:T(8,128)S(1)} %get-tuple-element.19), channel_id=1, source_target_pairs={{0,30},{2,0},{4,2},{6,4},{8,6},{10,8},{12,10},{14,12},{16,14},{18,... | collective-permute-start | bytes 516104 | tf_op jit(solution)/shard_map/ppermute | solution.py:22
  12.1 0.0 collective-permute-start
  12.1 6.2 %pack.1 = (f32[8,2,24,768]{3,2,1,0:T(8,128)}, f32[24,768]{1,0:T(8,128)}) custom-call(s32[1,768]{1,0:T(1,128)} %constant.20.clone.source_ref, f32[4608,24]{1,0:T(8,128)} %bitcast.3, f32[4608,24]{1,0:T(8,128)} %bitcast.4, f32[576,24]{1,0:T(8,128)} %bitcast.5), custom_call_target="tpu_custom_call" | custom-call | flops 4294967296 | bytes 8388608 | tf_op jit(solution)/shard_map/pack/pallas_call | solution.py:445
  18.4 0.0 collective-permute-done.1.refs_2_.refs_4_
  18.4 0.0 copy-start
  18.4 1.9 %collective-permute-done.refs_1_.refs_3_ = f32[2,12,1792]{2,1,0:T(8,128)S(1)} collective-permute-done((f32[2,12,1792]{2,1,0:T(8,128)S(1)}, f32[2,12,1792]{2,1,0:T(8,128)S(1)}, u32[]{:S(2)}, u32[]{:S(2)}) %collective-permute-start) | collective-permute-done | bytes 172064 | tf_op jit(solution)/shard_map/ppermute | solution.py:22
  20.3 0.0 copy-start.1
  20.3 0.0 copy-done
  20.3 0.7 %copy-done.1 = f32[2,12,1792]{2,1,0:T(8,128)} copy-done((f32[2,12,1792]{2,1,0:T(8,128)}, f32[2,12,1792]{2,1,0:T(8,128)S(1)}, u32[]{:S(2)}) %copy-start.1) | copy-done | bytes 172056
  21.0 10.1 %first_0.1 = (f32[144,640]{1,0:T(8,128)}, f32[2,2,24,384]{3,2,1,0:T(8,128)}) custom-call(f32[2,24,3456]{2,1,0:T(8,128)} %refs_0_.3, f32[2,12,1792]{2,1,0:T(8,128)} %copy-done.1, f32[2,12,1792]{2,1,0:T(8,128)} %copy-done, f32[8,2,24,768]{3,2,1,0:T(8,128)} %get-tuple-element.11.refs_3_.refs_5_, f32[24,768]{1,0:T(8,128)} %get-tuple-element.12.refs_4_.refs_6_, ...), custom_call_target="tpu_custom_call" | custom-call | flops 10737418240 | bytes 4194304 | tf_op jit(solution)/shard_map/first_0/pallas_call | solution.py:480
  31.1 1.5 %collective-permute-start.5 = (f32[2,2,24,384]{3,2,1,0:T(8,128)}, f32[2,2,24,384]{3,2,1,0:T(8,128)S(1)}, u32[]{:S(2)}, u32[]{:S(2)}) collective-permute-start(f32[2,2,24,384]{3,2,1,0:T(8,128)} %get-tuple-element.16), channel_id=1, source_target_pairs={{0,1},{1,0},{2,3},{3,2},{4,5},{5,4},{6,7},{7,6},{8,9},{9,8},{10,11... | collective-permute-start | bytes 442376 | tf_op jit(solution)/shard_map/ppermute | solution.py:22
  32.6 0.0 collective-permute-done.3.refs_2_
  32.6 0.0 copy-start.2
  32.6 0.0 collective-permute-done.2.refs_1_
  32.6 0.7 %copy-done.2 = f32[2,12,1664]{2,1,0:T(8,128)} copy-done((f32[2,12,1664]{2,1,0:T(8,128)}, f32[2,12,1664]{2,1,0:T(8,128)S(1)}, u32[]{:S(2)}) %copy-start.2) | copy-done | bytes 159768
  33.3 0.0 copy-start.3
  33.3 0.7 %copy-done.3 = f32[2,12,1664]{2,1,0:T(8,128)} copy-done((f32[2,12,1664]{2,1,0:T(8,128)}, f32[2,12,1664]{2,1,0:T(8,128)S(1)}, u32[]{:S(2)}) %copy-start.3) | copy-done | bytes 159768
  34.0 10.2 %first_1.1 = (f32[144,640]{1,0:T(8,128)}, f32[2,2,24,384]{3,2,1,0:T(8,128)}) custom-call(f32[2,24,3456]{2,1,0:T(8,128)} %refs_0_.3, f32[2,12,1664]{2,1,0:T(8,128)} %copy-done.3, f32[2,12,1664]{2,1,0:T(8,128)} %copy-done.2, f32[2,12,1792]{2,1,0:T(8,128)} %copy-done.1, f32[2,12,1792]{2,1,0:T(8,128)} %copy-done, ...), custom_call_target="tpu_custom_call" | custom-call | flops 10737418240 | bytes 4194304 | tf_op jit(solution)/shard_map/first_1/pallas_call | solution.py:480
  44.1 0.5 collective-permute-start.4
  44.6 0.0 collective-permute-done.5.refs_2_
  44.6 0.0 copy-start.4
  44.7 0.7 %copy-done.4 = f32[2,2,24,384]{3,2,1,0:T(8,128)} copy-done((f32[2,2,24,384]{3,2,1,0:T(8,128)}, f32[2,2,24,384]{3,2,1,0:T(8,128)S(1)}, u32[]{:S(2)}) %copy-start.4) | copy-done | bytes 147480
  45.3 9.8 %second_1.1.refs_10_ = f32[2,24,1792]{2,1,0:T(8,128)} custom-call(f32[144,640]{1,0:T(8,128)} %get-tuple-element.13.refs_0_, f32[144,640]{1,0:T(8,128)} %get-tuple-element.14.refs_1_, f32[2,2,24,384]{3,2,1,0:T(8,128)} %copy-done.4, f32[8,2,24,768]{3,2,1,0:T(8,128)} %get-tuple-element.11.refs_3_.refs_5_, f32[24,768]{1,0:T(8,128)} %get-tuple-element.12.refs_4_.refs_6_, ...), custom_call_target="tpu_custom_call" | custom-call | flops 10737418240 | bytes 4194304 | tf_op jit(solution)/shard_map/second_1/pallas_call | solution.py:499
  55.1 0.0 collective-permute-done.4.refs_2_
  55.1 0.0 copy-start.5
  55.1 0.6 copy-done.5
  55.8 10.1 %second_0.1 = f32[2,24,3456]{2,1,0:T(8,128)} custom-call(f32[144,640]{1,0:T(8,128)} %get-tuple-element.13.refs_0_, f32[144,640]{1,0:T(8,128)} %get-tuple-element.14.refs_1_, f32[2,2,24,384]{3,2,1,0:T(8,128)} %copy-done.5, f32[8,2,24,768]{3,2,1,0:T(8,128)} %get-tuple-element.11.refs_3_.refs_5_, f32[24,768]{1,0:T(8,128)} %get-tuple-element.12.refs_4_.refs_6_, ...), custom_call_target="tpu_custom_call" | custom-call | flops 10737418240 | bytes 4194304 | tf_op jit(solution)/shard_map/second_0/pallas_call | solution.py:499
Async XLA Ops:
  1.1 31.5 %collective-permute-start.3 = (f32[2,12,1664]{2,1,0:T(8,128)S(1)}, f32[2,12,1664]{2,1,0:T(8,128)S(1)}, u32[]{:S(2)}, u32[]{:S(2)}) collective-permute-start(f32[2,12,1664]{2,1,0:T(8,128)S(1)} %get-tuple-element.17), channel_id=1, source_target_pairs={{0,30},{2,0},{4,2},{6,4},{8,6},{10,8},{12,10},{14,12},{16,14},{18,... | collective-permute-start | bytes 479240 | tf_op jit(solution)/shard_map/ppermute | solution.py:22
  6.6 26.0 %collective-permute-start.2 = (f32[2,12,1664]{2,1,0:T(8,128)S(1)}, f32[2,12,1664]{2,1,0:T(8,128)S(1)}, u32[]{:S(2)}, u32[]{:S(2)}) collective-permute-start(f32[2,12,1664]{2,1,0:T(8,128)S(1)} %get-tuple-element.18), channel_id=1, source_target_pairs={{0,2},{2,4},{4,6},{6,8},{8,10},{10,12},{12,14},{14,16},{16,18},{18... | collective-permute-start | bytes 479240 | tf_op jit(solution)/shard_map/ppermute | solution.py:22
  7.7 10.7 %collective-permute-start.1 = (f32[2,12,1792]{2,1,0:T(8,128)S(1)}, f32[2,12,1792]{2,1,0:T(8,128)S(1)}, u32[]{:S(2)}, u32[]{:S(2)}) collective-permute-start(f32[2,12,1792]{2,1,0:T(8,128)S(1)} %get-tuple-element.19), channel_id=1, source_target_pairs={{0,30},{2,0},{4,2},{6,4},{8,6},{10,8},{12,10},{14,12},{16,14},{18,... | collective-permute-start | bytes 516104 | tf_op jit(solution)/shard_map/ppermute | solution.py:22
  12.1 8.1 %collective-permute-start = (f32[2,12,1792]{2,1,0:T(8,128)S(1)}, f32[2,12,1792]{2,1,0:T(8,128)S(1)}, u32[]{:S(2)}, u32[]{:S(2)}) collective-permute-start(f32[2,12,1792]{2,1,0:T(8,128)S(1)} %get-tuple-element.20), channel_id=1, source_target_pairs={{0,2},{2,4},{4,6},{6,8},{8,10},{10,12},{12,14},{14,16},{16,18},{18... | collective-permute-start | bytes 516104 | tf_op jit(solution)/shard_map/ppermute | solution.py:22
  18.4 1.9 %copy-start = (f32[2,12,1792]{2,1,0:T(8,128)}, f32[2,12,1792]{2,1,0:T(8,128)S(1)}, u32[]{:S(2)}) copy-start(f32[2,12,1792]{2,1,0:T(8,128)S(1)} %collective-permute-done.1.refs_2_.refs_4_) | copy-start | bytes 516100
  20.3 0.7 %copy-start.1 = (f32[2,12,1792]{2,1,0:T(8,128)}, f32[2,12,1792]{2,1,0:T(8,128)S(1)}, u32[]{:S(2)}) copy-start(f32[2,12,1792]{2,1,0:T(8,128)S(1)} %collective-permute-done.refs_1_.refs_3_) | copy-start | bytes 516100
  31.1 13.6 %collective-permute-start.5 = (f32[2,2,24,384]{3,2,1,0:T(8,128)}, f32[2,2,24,384]{3,2,1,0:T(8,128)S(1)}, u32[]{:S(2)}, u32[]{:S(2)}) collective-permute-start(f32[2,2,24,384]{3,2,1,0:T(8,128)} %get-tuple-element.16), channel_id=1, source_target_pairs={{0,1},{1,0},{2,3},{3,2},{4,5},{5,4},{6,7},{7,6},{8,9},{9,8},{10,11... | collective-permute-start | bytes 442376 | tf_op jit(solution)/shard_map/ppermute | solution.py:22
  32.6 0.7 %copy-start.2 = (f32[2,12,1664]{2,1,0:T(8,128)}, f32[2,12,1664]{2,1,0:T(8,128)S(1)}, u32[]{:S(2)}) copy-start(f32[2,12,1664]{2,1,0:T(8,128)S(1)} %collective-permute-done.3.refs_2_) | copy-start | bytes 479236
  33.3 0.7 %copy-start.3 = (f32[2,12,1664]{2,1,0:T(8,128)}, f32[2,12,1664]{2,1,0:T(8,128)S(1)}, u32[]{:S(2)}) copy-start(f32[2,12,1664]{2,1,0:T(8,128)S(1)} %collective-permute-done.2.refs_1_) | copy-start | bytes 479236
  44.1 11.0 %collective-permute-start.4 = (f32[2,2,24,384]{3,2,1,0:T(8,128)}, f32[2,2,24,384]{3,2,1,0:T(8,128)S(1)}, u32[]{:S(2)}, u32[]{:S(2)}) collective-permute-start(f32[2,2,24,384]{3,2,1,0:T(8,128)} %get-tuple-element.15), channel_id=1, source_target_pairs={{0,1},{1,0},{2,3},{3,2},{4,5},{5,4},{6,7},{7,6},{8,9},{9,8},{10,11... | collective-permute-start | bytes 442376 | tf_op jit(solution)/shard_map/ppermute | solution.py:22
  44.6 0.7 %copy-start.4 = (f32[2,2,24,384]{3,2,1,0:T(8,128)}, f32[2,2,24,384]{3,2,1,0:T(8,128)S(1)}, u32[]{:S(2)}) copy-start(f32[2,2,24,384]{3,2,1,0:T(8,128)S(1)} %collective-permute-done.5.refs_2_) | copy-start | bytes 442372
  55.1 0.7 copy-start.5

commit v2 on v1

v2 whole, which is shorter than its diff:
```python
import functools

import jax
import jax.numpy as jnp
import numpy as np
from jax import lax
from jax.experimental import pallas as pl
from jax.experimental.pallas import tpu as pltpu
from jax.sharding import PartitionSpec as P

courant_max = 1.6
collide_step = 0.2
lanes = 128
pack_mib, first_mib, second_mib = 24, 28, 24
bf16 = jnp.bfloat16
f32 = jnp.float32
dot = functools.partial(jnp.dot, preferred_element_type=f32)


def passed_along(value, axis, steps):
    count = lax.axis_size(axis)
    pairs = [(source, (source + steps) % count) for source in range(count)]
    return lax.ppermute(value, axis, pairs)


def cosine_table(count):
    freq = np.arange(count)[:, None]
    points = np.arange(count)[None, :]
    scale = np.where(freq == 0, np.sqrt(1.0 / count), np.sqrt(2.0 / count))
    return scale * np.cos(np.pi * (2.0 * points + 1.0) * freq / (2.0 * count))


def two_parts(table):
    high = np.asarray(table, np.float32).astype(bf16)
    return high, (table - high.astype(np.float64)).astype(np.float32).astype(bf16)


def courant_weights(count):
    speeds = np.arange(count) - (count - 1) / 2.0
    a = courant_max * np.abs(speeds) / ((count - 1) / 2.0)
    return np.stack([1.0 - 1.5 * a + 0.5 * a * a, 2.0 * a - a * a, 0.5 * (a * a - a)])


def sign(s, q):
    return -1.0 if ((s >> 1) & (q >> 1)) ^ (s & 1 & q) else 1.0


def block_table(count, q):
    c = cosine_table(count)
    half = count // 2
    return np.kron(c[q >> 1 :: 2, :half], c[q & 1 :: 2, :half])


def point_lanes(count):
    half = count // 2
    block = half * half
    rest = block - lanes
    source = np.full(5 * lanes, -1, np.int32)
    for s in range(4):
        for m in range(block):
            j, l = divmod(m, half)
            y = count - 1 - j if s >> 1 else j
            z = count - 1 - l if s & 1 else l
            if m < lanes:
                source[s * lanes + m] = y * count + z
            else:
                for copy in range(2):
                    source[4 * lanes + copy * 4 * rest + s * rest + m - lanes] = y * count + z
    return source


def mode_lanes(count):
    half = count // 2
    block = half * half
    rest = block - lanes
    source = np.full(6 * lanes, -1, np.int32)
    for q in range(4):
        for m in range(block):
            j, l = divmod(m, half)
            place = (2 * j + (q >> 1)) * count + 2 * l + (q & 1)
            if m < lanes:
                source[q * lanes + m] = place
            else:
                for copy in range(3):
                    source[(4 + q // 2) * lanes + copy * 2 * rest + (q % 2) * rest + m - lanes] = place
    return source


def inverse_tables(count):
    rest = (count // 2) ** 2 - lanes
    out = np.zeros((4, 4 * lanes, 2 * lanes), bf16)
    for q in range(4):
        table = block_table(count, q)
        wide = np.zeros((table.shape[0], 2 * lanes))
        wide[:, :lanes] = table[:, :lanes]
        for s in range(4):
            for copy in range(2):
                at = lanes + copy * 4 * rest + s * rest
                wide[:, at : at + rest] = sign(s, q) * table[:, lanes:]
        high, low = two_parts(wide)
        out[q, :lanes] = high[:lanes]
        out[q, lanes : 2 * lanes] = high[:lanes]
        out[q, 2 * lanes : 3 * lanes] = low[:lanes]
        for copy, part in enumerate((high, high, low)):
            at = 3 * lanes + copy * 2 * rest + (q % 2) * rest
            out[q, at : at + rest] = part[lanes:]
    return out


def forward_tables(count):
    rest = (count // 2) ** 2 - lanes
    out = np.zeros((4, 5 * lanes, 2 * lanes), bf16)
    for q in range(4):
        table = block_table(count, q).T
        wide = np.zeros((table.shape[0], 2 * lanes))
        wide[:, :lanes] = table[:, :lanes]
        for copy in range(3):
            at = lanes + copy * 2 * rest + (q % 2) * rest
            wide[:, at : at + rest] = table[:, lanes:]
        high, low = two_parts(wide)
        out[q, :lanes] = high[:lanes]
        out[q, lanes : 2 * lanes] = high[:lanes]
        out[q, 2 * lanes : 3 * lanes] = low[:lanes]
        for s in range(4):
            for at, part in ((3 * lanes, high), (3 * lanes + 4 * rest, high), (4 * lanes, low)):
                at = at + s * rest
                out[q, at : at + rest] = (sign(s, q) * part[lanes:].astype(np.float32)).astype(bf16)
    return out


def cells_together(cells):
    return max(n for n in (1, 2, 4) if cells % n == 0)


def row_tables(count, cells):
    c = cosine_table(count)
    result = []
    for table in (c, c.T):
        coarse, fine = two_parts(np.kron(np.eye(cells), table))
        upper = np.concatenate([coarse, coarse], axis=1)
        lower = np.concatenate([fine, np.zeros_like(fine)], axis=1)
        result.append(np.concatenate([upper, lower], axis=0))
    return np.stack(result)


def split(value):
    high = value.astype(bf16)
    return high, (value - high.astype(f32)).astype(bf16)


def lane_index():
    return lax.broadcasted_iota(jnp.int32, (1, lanes), 1)


def tile(value, at):
    return value[:, at * lanes : (at + 1) * lanes]


def crossed(v0, v1, v2, v3):
    t0, t1, t2, t3 = v0 + v1, v0 - v1, v2 + v3, v2 - v3
    return t0 + t2, t1 + t3, t0 - t2, t1 - t3


def along_rows(values, table, size):
    parts = [split(value) for value in values]
    found = []
    for at in range(0, values[0].shape[0], size):
        pieces = [jnp.concatenate([high[at : at + size], low[at : at + size]], axis=0) for high, low in parts]
        both = dot(table, jnp.concatenate(pieces, axis=1))
        found.append(both[:size] + both[size:])
    return found


def forward(value, table_ref, rest):
    mixed = crossed(*[tile(value, s) for s in range(4)])
    high, low = split(tile(value, 4))
    both = jnp.where(lane_index() < 4 * rest, high.astype(f32), low.astype(f32)).astype(bf16)
    found = []
    for q in range(4):
        q_high, q_low = split(mixed[q])
        found.append(dot(jnp.concatenate([q_high, q_low, q_high, both, high], axis=1), table_ref[q]))
    return jnp.concatenate(
        [tile(v, 0) for v in found] + [tile(found[0], 1) + tile(found[1], 1), tile(found[2], 1) + tile(found[3], 1)],
        axis=1,
    )


def inverse_plane(modes, table_ref, rest):
    low_lanes = (lane_index() >= 2 * rest) & (lane_index() < 4 * rest)
    both = []
    for pair in range(2):
        value = tile(modes, 4 + pair)
        high = value.astype(bf16).astype(f32)
        both.append(jnp.where(low_lanes, value - high, high).astype(bf16))
    found = []
    for q in range(4):
        high, low = split(tile(modes, q))
        found.append(dot(jnp.concatenate([high, low, high, both[q // 2]], axis=1), table_ref[q]))
    main = crossed(*[tile(v, 0) for v in found])
    last = (tile(found[0], 1) + tile(found[1], 1)) + (tile(found[2], 1) + tile(found[3], 1))
    return jnp.concatenate(list(main) + [last], axis=1)


def collide(field_ref, modes_ref, sum_ref, kernel_ref, loss_ref, inverse_ref, forward_ref, rows_ref, count, rest, most):
    rows = field_ref.shape[0]
    cells = rows // count
    terms = kernel_ref.shape[0]
    together = max(n for n in range(1, most + 1) if terms % n == 0)
    wide = 5 * lanes
    size = rows_ref.shape[2] // 2

    def scaled(factor):
        modes = modes_ref[...].reshape(cells, count, 6 * lanes)
        return (modes * factor[None]).reshape(rows, 6 * lanes)

    for k, part in enumerate(along_rows([forward(field_ref[...], forward_ref, rest)], rows_ref[0], size)):
        modes_ref[k * size : (k + 1) * size] = part
    plane = inverse_plane(scaled(loss_ref[...]), inverse_ref, rest)
    for k, part in enumerate(along_rows([plane], rows_ref[1], size)):
        at = slice(k * size, (k + 1) * size)
        sum_ref[at] = -field_ref[at] * part

    def term(step, carry):
        factors = [kernel_ref[together * step + k, side] for k in range(together) for side in range(2)]
        plane = inverse_plane(jnp.concatenate([scaled(f) for f in factors], axis=0), inverse_ref, rest)
        planes = [plane[k * rows : (k + 1) * rows] for k in range(2 * together)]
        for k, part in enumerate(along_rows(planes, rows_ref[1], size)):
            at = slice(k * size, (k + 1) * size)
            total = sum_ref[at]
            for pair in range(together):
                lane = 2 * pair * wide
                total = total + part[:, lane : lane + wide] * part[:, lane + wide : lane + 2 * wide]
            sum_ref[at] = total
        return carry

    lax.fori_loop(0, terms // together, term, 0)
    field_ref[...] = field_ref[...] + collide_step * sum_ref[...]


def one_hot(source_row, rows):
    index = lax.broadcasted_iota(jnp.int32, (rows, source_row.shape[1]), 0)
    return jnp.where(index == source_row, 1.0, 0.0).astype(bf16)


def moved(value, table):
    high, low = split(value)
    both = dot(jnp.concatenate([high, low], axis=0), table)
    return both[: value.shape[0]] + both[value.shape[0] :]


def pack_kernel(count, source_ref, move_ref, a_ref, b_ref, loss_ref, out_ref, loss_out_ref, moves_ref, table_ref):
    @pl.when(pl.program_id(0) == 0)
    def _():
        table_ref[...] = one_hot(source_ref[...], count * count)

    for k in range(moves_ref.shape[0]):
        moves_ref[k] = one_hot(move_ref[k], 5 * lanes)

    def rows_of(ref):
        rows = ref.shape[0] // count
        return jnp.concatenate([ref[pl.ds(k, rows, stride=count), :] for k in range(count)], axis=1)

    terms = out_ref.shape[0]
    both = jnp.concatenate([rows_of(a_ref), rows_of(b_ref)], axis=0)
    both = moved(both, table_ref[...]).reshape(2, terms, count, 6 * lanes)
    for side in range(2):
        out_ref[:, side] = both[side]

    @pl.when(pl.program_id(0) == 0)
    def _():
        loss_out_ref[...] = moved(rows_of(loss_ref), table_ref[...])


class Cells:
    def __init__(self, cells_x, count, ys):
        plane = count * count
        self.count = count
        self.parts = [
            [(x, y) for x in range(cells_x) for y in ys if y * plane % lanes == shift] for shift in (0, lanes // 2)
        ]
        self.order = self.parts[0] + self.parts[1]
        self.size = len(self.order) * count

    def rows(self, x, y):
        at = self.order.index((x, y)) * self.count
        return slice(at, at + self.count)

    def part_rows(self, k):
        at = k * len(self.parts[0]) * self.count
        return slice(at, at + len(self.parts[k]) * self.count)


def first_kernel(
    count, rest, cells, cells_y,
    density_ref, below_ref, above_ref, kernel_ref, loss_ref, inverse_ref, forward_ref, rows_ref, speed_ref, moves_ref,
    field_ref, up_ref, down_ref, modes_ref, sum_ref, rim_ref,
):
    cells_x = density_ref.shape[0]
    middle = count // 2
    plane = count * count
    for i in range(2):
        rim_ref[i, :middle] = above_ref[i]
        rim_ref[i, middle:] = below_ref[i]
    positive = lax.broadcasted_iota(jnp.int32, (count, 1), 0) >= middle

    def behind(x):
        return density_ref[x] if x >= 0 else rim_ref[x + 2]

    def ahead(x):
        return density_ref[x] if x < cells_x else rim_ref[x - cells_x]

    w0, w1, w2 = [speed_ref[:, k : k + 1] for k in range(3)]
    moved_on = []
    for x in range(cells_x):
        near = jnp.where(positive, behind(x - 1), ahead(x + 1))
        far = jnp.where(positive, behind(x - 2), ahead(x + 2))
        moved_on.append(w0 * density_ref[x] + w1 * near + w2 * far)
    for k, part in enumerate(cells.parts):
        starts = [(x, y * plane // lanes * lanes) for x, y in part]
        values = jnp.concatenate([moved_on[x][:, at : at + 5 * lanes] for x, at in starts], axis=0)
        field_ref[cells.part_rows(k)] = moved(values, moves_ref[k])
    collide(field_ref, modes_ref, sum_ref, kernel_ref, loss_ref, inverse_ref, forward_ref, rows_ref, count, rest, 2)
    for x in range(cells_x):
        for k in range(2):
            up_ref[x, k] = field_ref[cells.rows(x, cells_y - 2 + k), 2 * lanes :]
            down_ref[x, k, :, : 2 * lanes] = field_ref[cells.rows(x, k), : 2 * lanes]
            down_ref[x, k, :, 2 * lanes :] = field_ref[cells.rows(x, k), 4 * lanes :]


def sweep_y(given_ref, below_ref, above_ref, speed_ref, field_ref, everything, cells, cells_y, rest):
    backward_last = (lane_index() // (2 * rest)) % 2 == 1

    def cell(x, y, part):
        if y < 0:
            return below_ref[x, y + 2, :, (part - 2) * lanes : (part - 1) * lanes]
        if y >= cells_y:
            at = part if part < 2 else 2
            return above_ref[x, y - cells_y, :, at * lanes : (at + 1) * lanes]
        return given_ref[everything.rows(x, y), part * lanes : (part + 1) * lanes]

    for x, y in cells.order:
        for part in range(5):
            w0, w1, w2 = [speed_ref[k : k + 1, part * lanes : (part + 1) * lanes] for k in range(3)]
            if part < 2:
                near, far = cell(x, y + 1, part), cell(x, y + 2, part)
            elif part < 4:
                near, far = cell(x, y - 1, part), cell(x, y - 2, part)
            else:
                near = jnp.where(backward_last, cell(x, y - 1, part), cell(x, y + 1, part))
                far = jnp.where(backward_last, cell(x, y - 2, part), cell(x, y + 2, part))
            field_ref[cells.rows(x, y), part * lanes : (part + 1) * lanes] = (
                w0 * cell(x, y, part) + w1 * near + w2 * far
            )


def inner_kernel(
    count, rest, everything, cells, cells_y,
    given_ref, kernel_ref, loss_ref, inverse_ref, forward_ref, rows_ref, speed_ref,
    field_ref, modes_ref, sum_ref,
):
    sweep_y(given_ref, None, None, speed_ref, field_ref, everything, cells, cells_y, rest)
    collide(field_ref, modes_ref, sum_ref, kernel_ref, loss_ref, inverse_ref, forward_ref, rows_ref, count, rest, 4)


def outer_kernel(
    count, rest, everything, inner, cells, cells_y,
    given_ref, inner_ref, below_ref, above_ref, kernel_ref, loss_ref, inverse_ref, forward_ref, rows_ref, speed_ref,
    moves_ref,
    out_ref, field_ref, modes_ref, sum_ref,
):
    plane = count * count
    sweep_y(given_ref, below_ref, above_ref, speed_ref, field_ref, everything, cells, cells_y, rest)
    collide(field_ref, modes_ref, sum_ref, kernel_ref, loss_ref, inverse_ref, forward_ref, rows_ref, count, rest, 2)
    pieces = {}
    for k in range(2):
        values = [field_ref[cells.part_rows(k)], inner_ref[inner.part_rows(k)]]
        natural = moved(jnp.concatenate(values, axis=0), moves_ref[2 + k])
        for i, place in enumerate(cells.parts[k] + inner.parts[k]):
            pieces[place] = natural[i * count : (i + 1) * count]
    for x in range(out_ref.shape[0]):
        filled = {}
        for y in range(cells_y):
            first = y * plane // lanes
            for t in range(5):
                value = tile(pieces[x, y], t)
                filled[first + t] = filled[first + t] + value if first + t in filled else value
        for t in range(out_ref.shape[2] // lanes):
            out_ref[x, :, t * lanes : (t + 1) * lanes] = filled[t]


def body(density, gains_a, gains_b, loss_rates):
    cells_x, count, width = density.shape
    terms = gains_a.shape[0]
    middle = count // 2
    plane = count * count
    cells_y = width // plane
    rest = middle * middle - lanes
    everything = Cells(cells_x, count, range(cells_y))
    inner = Cells(cells_x, count, range(2, cells_y - 2))
    outer = Cells(cells_x, count, [*range(2), *range(cells_y - 2, cells_y)])
    points = point_lanes(count)
    moves = np.full((4, 1, 5 * lanes), -1, np.int32)
    for k in range(2):
        shift = k * lanes // 2
        moves[k, 0] = np.where(points >= 0, points + shift, -1)
        for lane in range(4 * lanes + 4 * rest):
            moves[2 + k, 0, points[lane] + shift] = lane
    weights = courant_weights(count)
    lane_speed = np.where(points >= 0, weights[:, points // count], 0.0).astype(np.float32)
    lane_speed = jnp.asarray(lane_speed)
    row_speed = jnp.asarray(weights.T.astype(np.float32))
    group = min(cells_together(c.size // count) for c in (everything, inner, outer))
    tables = [jnp.asarray(t) for t in (inverse_tables(count), forward_tables(count), row_tables(count, group))]

    def params(mib):
        return pltpu.CompilerParams(vmem_limit_bytes=mib << 20)

    def scratch(cells):
        return [pltpu.VMEM((cells.size, k * lanes), f32) for k in (6, 5)]

    def cost(cells):
        return pl.CostEstimate(flops=cells.size << 27, bytes_accessed=4 << 20, transcendentals=0)

    below = passed_along(density[-2:, middle:], "gx", 1)
    above = passed_along(density[:2, :middle], "gx", -1)
    steps = 2 if terms % 2 == 0 else 1
    taken = terms // steps
    gain_spec = pl.BlockSpec((taken * plane, count), lambda i: (i, 0))
    packed, packed_loss, move_tables = pl.pallas_call(
        functools.partial(pack_kernel, count),
        grid=(steps,),
        in_specs=[
            pl.BlockSpec((1, 6 * lanes), lambda i: (0, 0)),
            pl.BlockSpec((4 // steps, 1, 5 * lanes), lambda i: (i, 0, 0)),
            gain_spec,
            gain_spec,
            pl.BlockSpec((plane, count), lambda i: (0, 0)),
        ],
        out_specs=[
            pl.BlockSpec((taken, 2, count, 6 * lanes), lambda i: (i, 0, 0, 0)),
            pl.BlockSpec((count, 6 * lanes), lambda i: (0, 0)),
            pl.BlockSpec((4 // steps, 5 * lanes, 5 * lanes), lambda i: (i, 0, 0)),
        ],
        out_shape=(
            jax.ShapeDtypeStruct((terms, 2, count, 6 * lanes), f32),
            jax.ShapeDtypeStruct((count, 6 * lanes), f32),
            jax.ShapeDtypeStruct((4, 5 * lanes, 5 * lanes), bf16),
        ),
        scratch_shapes=[pltpu.VMEM((plane, 6 * lanes), bf16)],
        compiler_params=params(pack_mib),
        cost_estimate=pl.CostEstimate(flops=4 << 30, bytes_accessed=8 << 20, transcendentals=0),
        name="pack",
    )(
        jnp.asarray(mode_lanes(count)[None]),
        jnp.asarray(moves),
        gains_a.reshape(-1, count),
        gains_b.reshape(-1, count),
        loss_rates.reshape(-1, count),
    )
    rim_shape = jax.ShapeDtypeStruct((cells_x, 2, count, 3 * lanes), f32)
    field, up, down = pl.pallas_call(
        functools.partial(first_kernel, count, rest, everything, cells_y),
        out_shape=(jax.ShapeDtypeStruct((everything.size, 5 * lanes), f32), rim_shape, rim_shape),
        scratch_shapes=scratch(everything) + [pltpu.VMEM((2, count, width), f32)],
        compiler_params=params(first_mib),
        cost_estimate=cost(everything),
        name="first",
    )(density, below, above, packed, packed_loss, *tables, row_speed, move_tables)
    y_below = passed_along(up, "gy", 1)
    y_above = passed_along(down, "gy", -1)
    inner_field = pl.pallas_call(
        functools.partial(inner_kernel, count, rest, everything, inner, cells_y),
        out_shape=jax.ShapeDtypeStruct((inner.size, 5 * lanes), f32),
        scratch_shapes=scratch(inner),
        compiler_params=params(second_mib),
        cost_estimate=cost(inner),
        name="inner",
    )(field, packed, packed_loss, *tables, lane_speed)
    return pl.pallas_call(
        functools.partial(outer_kernel, count, rest, everything, inner, outer, cells_y),
        out_shape=jax.ShapeDtypeStruct(density.shape, f32),
        scratch_shapes=[pltpu.VMEM((outer.size, 5 * lanes), f32)] + scratch(outer),
        compiler_params=params(second_mib),
        cost_estimate=cost(outer),
        name="outer",
    )(field, inner_field, y_below, y_above, packed, packed_loss, *tables, lane_speed, move_tables)


def solution(mesh):
    in_specs = (P("gx", None, "gy"), P(), P(), P())
    out_specs = P("gx", None, "gy")
    return jax.shard_map(body, mesh=mesh, in_specs=in_specs, out_specs=out_specs, check_vma=False)
```

time: 66.1 us -> 45.5 us (0.69)
  Pallas kernels: 46.4 us -> 29.8 us
  starting transfers between devices: 12 us -> 7.59 us
  local copies, waits for them, and re-layouts: 5.51 us -> 6.91 us
  waiting for transfers between devices: 1.89 us -> 0.83 us
    pallas_call x4 -> x3, Pallas kernels: 40.1 us -> 25.6 us  [the longest x1 11.8 us: body(): pl.pallas_call(functools.partial(first_kernel, count, rest, everything, c...]
    ppermute x6 -> x4, starting transfers between devices: 12 us -> 7.59 us  [passed_along(): return lax.ppermute(value, axis, pairs)]
    unnamed x12 -> x22, local copies, waits for them, and re-layouts: 3.37 us -> 5.7 us
    pallas_call x1, Pallas kernels: 6.25 us -> 4.16 us  [body(): pl.pallas_call(functools.partial(pack_kernel, count), grid=(steps,), in_s...]
    ppermute x6 -> x4, waiting for transfers between devices: 1.89 us -> 0.83 us  [passed_along(): return lax.ppermute(value, axis, pairs)]
    slice x2 -> x1, local copies, waits for them, and re-layouts: 2.15 us -> 1.21 us  [body(): above = passed_along(density[:2, :middle], 'gx', -1)]
  transfers between devices with their start and end apart: 6 -> 4, of which waited for: 1 -> 2; matrix products, arithmetic and copies ran while one was open for 2% -> 0% of each run, Pallas kernels for 55% -> 19%
where the time goes in v2:
time: 45.5 us; the launch traced here: 45.2 us
  Pallas kernels  29.8 us (65%)
  starting transfers between devices  7.59 us (17%)
  local copies, waits for them, and re-layouts  6.91 us (15%)
  waiting for transfers between devices  0.83 us (2%)
    pallas_call x1, Pallas kernels, body(): pl.pallas_call(functools.partial(first_kernel, count, rest, everything, c...  11.8 us
    pallas_call x1, Pallas kernels, body(): pl.pallas_call(functools.partial(outer_kernel, count, rest, everything, i...  9.41 us
    ppermute x4, starting transfers between devices, passed_along(): return lax.ppermute(value, axis, pairs)  7.59 us
    unnamed x22, local copies, waits for them, and re-layouts  5.7 us
    pallas_call x1, Pallas kernels, body(): pl.pallas_call(functools.partial(inner_kernel, count, rest, everything, i...  4.39 us
    pallas_call x1, Pallas kernels, body(): pl.pallas_call(functools.partial(pack_kernel, count), grid=(steps,), in_s...  4.16 us
    slice x1, local copies, waits for them, and re-layouts, body(): above = passed_along(density[:2, :middle], 'gx', -1)  1.21 us
  transfers between devices with their start and end apart: 4, of which 2 were waited for; matrix products, arithmetic and copies ran while one was open for 0% of the time, Pallas kernels for 19%

profile of v2, /device:TPU:0, one launch (start us, length us, event | category | flops | bytes accessed | tf_op | source)
XLA Modules:
  0.0 45.2 jit_solution(10545275896365461951)
XLA Ops:
  0.0 1.2 %fusion = (f32[2,12,3456]{2,1,0:T(8,128)S(1)}, f32[2,12,3456]{2,1,0:T(8,128)S(1)}) fusion(f32[2,24,3456]{2,1,0:T(8,128)} %density_ref.1), kind=kLoop, calls=%fused_computation | loop fusion | bytes 1327104 | tf_op jit(solution)/shard_map/slice | solution.py:425
  1.2 5.5 %collective-permute-start.1 = (f32[2,12,3456]{2,1,0:T(8,128)S(1)}, f32[2,12,3456]{2,1,0:T(8,128)S(1)}, u32[]{:S(2)}, u32[]{:S(2)}) collective-permute-start(f32[2,12,3456]{2,1,0:T(8,128)S(1)} %get-tuple-element.17), channel_id=1, source_target_pairs={{0,30},{2,0},{4,2},{6,4},{8,6},{10,8},{12,10},{14,12},{16,14},{18,... | collective-permute-start | bytes 995336 | tf_op jit(solution)/shard_map/ppermute | solution.py:23
  6.7 0.0 collective-permute-start
  6.7 0.0 copy-start.1
  6.7 1.7 %copy-done.1 = f32[8,24,24,24]{3,2,1,0:T(8,128)S(1)} copy-done((f32[8,24,24,24]{3,2,1,0:T(8,128)S(1)}, f32[8,24,24,24]{3,2,1,0:T(8,128)}, u32[]{:S(2)}) %copy-start.1) | copy-done | bytes 442392
  8.4 0.0 copy-start.2
  8.4 1.7 %copy-done.2 = f32[8,24,24,24]{3,2,1,0:T(8,128)S(1)} copy-done((f32[8,24,24,24]{3,2,1,0:T(8,128)S(1)}, f32[8,24,24,24]{3,2,1,0:T(8,128)}, u32[]{:S(2)}) %copy-start.2) | copy-done | bytes 442392
  10.0 0.0 copy-start.3
  10.0 1.0 %copy-done.3 = f32[24,24,24]{2,1,0:T(8,128)S(1)} copy-done((f32[24,24,24]{2,1,0:T(8,128)S(1)}, f32[24,24,24]{2,1,0:T(8,128)}, u32[]{:S(2)}) %copy-start.3) | copy-done | bytes 55320
  11.0 0.0 copy-start.9
  11.0 0.7 %copy-done.9 = s32[4,1,640]{2,1,0:T(1,128)S(1)} copy-done((s32[4,1,640]{2,1,0:T(1,128)S(1)}, s32[4,1,640]{2,1,0:T(1,128)}, u32[]{:S(2)}) %copy-start.9) | copy-done | bytes 10264
  11.7 0.0 copy-start.10
  11.7 0.7 %copy-done.10 = s32[1,768]{1,0:T(1,128)S(1)} copy-done((s32[1,768]{1,0:T(1,128)S(1)}, s32[1,768]{1,0:T(1,128)}, u32[]{:S(2)}) %copy-start.10) | copy-done | bytes 3096
  12.4 0.0 copy-start
  12.4 0.0 copy-start.7
  12.4 4.2 %pack.1 = (f32[8,2,24,768]{3,2,1,0:T(8,128)S(1)}, f32[24,768]{1,0:T(8,128)S(1)}, bf16[4,640,640]{2,1,0:T(8,128)(2,1)S(1)}) custom-call(s32[1,768]{1,0:T(1,128)S(1)} %copy-done.10, s32[4,1,640]{2,1,0:T(1,128)S(1)} %copy-done.9, f32[4608,24]{1,0:T(8,128)S(1)} %bitcast.3, f32[4608,24]{1,0:T(8,128)S(1)} %bitcast.4, f32[576,24]{1,0:T(8,128)S(1)} %bitcast.5), custom_call_target="tpu_custom_call" | custom-call | flops 4294967296 | bytes 8388608 | tf_op jit(solution)/shard_map/pack/pallas_call | solution.py:429
  16.6 0.0 collective-permute-done.1.above_ref
  16.6 0.5 %collective-permute-done.below_ref = f32[2,12,3456]{2,1,0:T(8,128)S(1)} collective-permute-done((f32[2,12,3456]{2,1,0:T(8,128)S(1)}, f32[2,12,3456]{2,1,0:T(8,128)S(1)}, u32[]{:S(2)}, u32[]{:S(2)}) %collective-permute-start) | collective-permute-done | bytes 331808 | tf_op jit(solution)/shard_map/ppermute | solution.py:23
  17.1 0.0 copy-done
  17.1 0.0 copy-done.4
  17.1 0.0 copy-done.5
  17.1 0.0 copy-done.6
  17.2 0.0 copy-done.7
  17.2 0.0 copy-start.8
  17.2 11.8 %first.1 = (f32[288,640]{1,0:T(8,128)S(1)}, f32[2,2,24,384]{3,2,1,0:T(8,128)S(1)}, f32[2,2,24,384]{3,2,1,0:T(8,128)S(1)}) custom-call(f32[2,24,3456]{2,1,0:T(8,128)S(1)} %copy-done, f32[2,12,3456]{2,1,0:T(8,128)S(1)} %collective-permute-done.below_ref, f32[2,12,3456]{2,1,0:T(8,128)S(1)} %collective-permute-done.1.above_ref, ...), custom_call_target="tpu_custom_call" | custom-call | flops 38654705664 | bytes 4194304 | tf_op jit(solution)/shard_map/first/pallas_call | solution.py:461
  29.0 1.6 %collective-permute-start.2 = (f32[2,2,24,384]{3,2,1,0:T(8,128)S(1)}, f32[2,2,24,384]{3,2,1,0:T(8,128)S(1)}, u32[]{:S(2)}, u32[]{:S(2)}) collective-permute-start(f32[2,2,24,384]{3,2,1,0:T(8,128)S(1)} %get-tuple-element.15), channel_id=1, source_target_pairs={{0,1},{1,0},{2,3},{3,2},{4,5},{5,4},{6,7},{7,6},{8,9},{9,8},{10,11... | collective-permute-start | bytes 442376 | tf_op jit(solution)/shard_map/ppermute | solution.py:23
  30.6 0.5 %collective-permute-start.3 = (f32[2,2,24,384]{3,2,1,0:T(8,128)S(1)}, f32[2,2,24,384]{3,2,1,0:T(8,128)S(1)}, u32[]{:S(2)}, u32[]{:S(2)}) collective-permute-start(f32[2,2,24,384]{3,2,1,0:T(8,128)S(1)} %get-tuple-element.16), channel_id=1, source_target_pairs={{0,1},{1,0},{2,3},{3,2},{4,5},{5,4},{6,7},{7,6},{8,9},{9,8},{10,11... | collective-permute-start | bytes 442376 | tf_op jit(solution)/shard_map/ppermute | solution.py:23
  31.1 0.0 copy-done.8
  31.1 4.4 %inner.1.inner_ref = f32[96,640]{1,0:T(8,128)S(1)} custom-call(f32[288,640]{1,0:T(8,128)S(1)} %get-tuple-element.14.given_ref, f32[8,2,24,768]{3,2,1,0:T(8,128)S(1)} %get-tuple-element.11.kernel_ref, f32[24,768]{1,0:T(8,128)S(1)} %get-tuple-element.12.loss_ref, bf16[4,512,256]{2,1,0:T(8,128)(2,1)S(1)} %copy-done.5, bf16[4,640,256]{2,1,0:T(8,128)(2,1)S(1)} %copy-done.4, ...), custom_call_target="tpu_custom_call" | custom-call | flops 12884901888 | bytes 4194304 | tf_op jit(solution)/shard_map/inner/pallas_call | solution.py:471
  35.5 0.0 collective-permute-done.2.below_ref
  35.5 0.3 collective-permute-done.3.above_ref
  35.8 9.4 %outer.1 = f32[2,24,3456]{2,1,0:T(8,128)} custom-call(f32[288,640]{1,0:T(8,128)S(1)} %get-tuple-element.14.given_ref, f32[96,640]{1,0:T(8,128)S(1)} %inner.1.inner_ref, f32[2,2,24,384]{3,2,1,0:T(8,128)S(1)} %collective-permute-done.2.below_ref, f32[2,2,24,384]{3,2,1,0:T(8,128)S(1)} %collective-permute-done.3.above_ref, ...), custom_call_target="tpu_custom_call" | custom-call | flops 25769803776 | bytes 4194304 | tf_op jit(solution)/shard_map/outer/pallas_call | solution.py:479
  (3 shorter events, 0.0 us)
Async XLA Ops:
  1.2 15.4 %collective-permute-start.1 = (f32[2,12,3456]{2,1,0:T(8,128)S(1)}, f32[2,12,3456]{2,1,0:T(8,128)S(1)}, u32[]{:S(2)}, u32[]{:S(2)}) collective-permute-start(f32[2,12,3456]{2,1,0:T(8,128)S(1)} %get-tuple-element.17), channel_id=1, source_target_pairs={{0,30},{2,0},{4,2},{6,4},{8,6},{10,8},{12,10},{14,12},{16,14},{18,... | collective-permute-start | bytes 995336 | tf_op jit(solution)/shard_map/ppermute | solution.py:23
  6.7 10.4 %collective-permute-start = (f32[2,12,3456]{2,1,0:T(8,128)S(1)}, f32[2,12,3456]{2,1,0:T(8,128)S(1)}, u32[]{:S(2)}, u32[]{:S(2)}) collective-permute-start(f32[2,12,3456]{2,1,0:T(8,128)S(1)} %get-tuple-element.18), channel_id=1, source_target_pairs={{0,2},{2,4},{4,6},{6,8},{8,10},{10,12},{12,14},{14,16},{16,18},{18... | collective-permute-start | bytes 995336 | tf_op jit(solution)/shard_map/ppermute | solution.py:23
  6.7 1.7 %copy-start.1 = (f32[8,24,24,24]{3,2,1,0:T(8,128)S(1)}, f32[8,24,24,24]{3,2,1,0:T(8,128)}, u32[]{:S(2)}) copy-start(f32[8,24,24,24]{3,2,1,0:T(8,128)} %param.12) | copy-start | bytes 1327108
  8.4 1.7 %copy-start.2 = (f32[8,24,24,24]{3,2,1,0:T(8,128)S(1)}, f32[8,24,24,24]{3,2,1,0:T(8,128)}, u32[]{:S(2)}) copy-start(f32[8,24,24,24]{3,2,1,0:T(8,128)} %param.13) | copy-start | bytes 1327108
  10.0 1.0 %copy-start.3 = (f32[24,24,24]{2,1,0:T(8,128)S(1)}, f32[24,24,24]{2,1,0:T(8,128)}, u32[]{:S(2)}) copy-start(f32[24,24,24]{2,1,0:T(8,128)} %param.14) | copy-start | bytes 165892
  11.0 0.7 %copy-start.9 = (s32[4,1,640]{2,1,0:T(1,128)S(1)}, s32[4,1,640]{2,1,0:T(1,128)}, u32[]{:S(2)}) copy-start(s32[4,1,640]{2,1,0:T(1,128)} %constant.20.clone.move_ref) | copy-start | bytes 30724
  11.7 0.7 %copy-start.10 = (s32[1,768]{1,0:T(1,128)S(1)}, s32[1,768]{1,0:T(1,128)}, u32[]{:S(2)}) copy-start(s32[1,768]{1,0:T(1,128)} %constant.19.clone.source_ref) | copy-start | bytes 9220
  12.4 4.7 %copy-start = (f32[2,24,3456]{2,1,0:T(8,128)S(1)}, f32[2,24,3456]{2,1,0:T(8,128)}, u32[]{:S(2)}) copy-start(f32[2,24,3456]{2,1,0:T(8,128)} %density_ref.1) | copy-start | bytes 1990660
  12.4 4.7 %copy-start.4 = (bf16[4,640,256]{2,1,0:T(8,128)(2,1)S(1)}, bf16[4,640,256]{2,1,0:T(8,128)(2,1)}, u32[]{:S(2)}) copy-start(bf16[4,640,256]{2,1,0:T(8,128)(2,1)} %constant.17.clone.forward_ref) | copy-start | bytes 3932164
  12.4 4.7 %copy-start.5 = (bf16[4,512,256]{2,1,0:T(8,128)(2,1)S(1)}, bf16[4,512,256]{2,1,0:T(8,128)(2,1)}, u32[]{:S(2)}) copy-start(bf16[4,512,256]{2,1,0:T(8,128)(2,1)} %constant.16.clone.inverse_ref) | copy-start | bytes 3145732
  12.4 4.7 %copy-start.6 = (bf16[2,192,192]{2,1,0:T(8,128)(2,1)S(1)}, bf16[2,192,192]{2,1,0:T(8,128)(2,1)}, u32[]{:S(2)}) copy-start(bf16[2,192,192]{2,1,0:T(8,128)(2,1)} %constant.18.clone.rows_ref) | copy-start | bytes 442372
  12.4 4.8 %copy-start.7 = (f32[24,3]{1,0:T(8,128)S(1)}, f32[24,3]{1,0:T(8,128)}, u32[]{:S(2)}) copy-start(f32[24,3]{1,0:T(8,128)} %constant.15.clone.speed_ref) | copy-start | bytes 868
  17.2 14.0 %copy-start.8 = (f32[3,640]{1,0:T(4,128)S(1)}, f32[3,640]{1,0:T(4,128)}, u32[]{:S(2)}) copy-start(f32[3,640]{1,0:T(4,128)} %constant.14.clone.speed_ref) | copy-start | bytes 23044
  29.0 6.5 %collective-permute-start.2 = (f32[2,2,24,384]{3,2,1,0:T(8,128)S(1)}, f32[2,2,24,384]{3,2,1,0:T(8,128)S(1)}, u32[]{:S(2)}, u32[]{:S(2)}) collective-permute-start(f32[2,2,24,384]{3,2,1,0:T(8,128)S(1)} %get-tuple-element.15), channel_id=1, source_target_pairs={{0,1},{1,0},{2,3},{3,2},{4,5},{5,4},{6,7},{7,6},{8,9},{9,8},{10,11... | collective-permute-start | bytes 442376 | tf_op jit(solution)/shard_map/ppermute | solution.py:23
  30.6 5.2 %collective-permute-start.3 = (f32[2,2,24,384]{3,2,1,0:T(8,128)S(1)}, f32[2,2,24,384]{3,2,1,0:T(8,128)S(1)}, u32[]{:S(2)}, u32[]{:S(2)}) collective-permute-start(f32[2,2,24,384]{3,2,1,0:T(8,128)S(1)} %get-tuple-element.16), channel_id=1, source_target_pairs={{0,1},{1,0},{2,3},{3,2},{4,5},{5,4},{6,7},{7,6},{8,9},{9,8},{10,11... | collective-permute-start | bytes 442376 | tf_op jit(solution)/shard_map/ppermute | solution.py:23

commit v3 on v2

--- a/solution.py
+++ b/solution.py
@@ -206,7 +206,7 @@
     cells = rows // count
     terms = kernel_ref.shape[0]
     together = max(n for n in range(1, most + 1) if terms % n == 0)
-    wide = 5 * lanes
+    main = 4 * lanes
     size = rows_ref.shape[2] // 2
 
     def scaled(factor):
@@ -223,14 +223,22 @@
     def term(step, carry):
         factors = [kernel_ref[together * step + k, side] for k in range(together) for side in range(2)]
         plane = inverse_plane(jnp.concatenate([scaled(f) for f in factors], axis=0), inverse_ref, rest)
-        planes = [plane[k * rows : (k + 1) * rows] for k in range(2 * together)]
-        for k, part in enumerate(along_rows(planes, rows_ref[1], size)):
+        pairs = []
+        for k in range(together):
+            first, second = [plane[(2 * k + side) * rows : (2 * k + side + 1) * rows] for side in range(2)]
+            shared = jnp.where(lane_index() < 4 * rest, tile(first, 4), tile(second, 4))
+            pairs.append(jnp.concatenate([first[:, :main], second[:, :main], shared], axis=1))
+        for k, part in enumerate(along_rows(pairs, rows_ref[1], size)):
             at = slice(k * size, (k + 1) * size)
-            total = sum_ref[at]
+            total = sum_ref[at, :main]
+            last = sum_ref[at, main:]
             for pair in range(together):
-                lane = 2 * pair * wide
-                total = total + part[:, lane : lane + wide] * part[:, lane + wide : lane + 2 * wide]
-            sum_ref[at] = total
+                lane = pair * (2 * main + lanes)
+                total = total + part[:, lane : lane + main] * part[:, lane + main : lane + 2 * main]
+                shared = part[:, lane + 2 * main : lane + 2 * main + lanes]
+                last = last + shared * pltpu.roll(shared, 4 * rest, 1)
+            sum_ref[at, :main] = total
+            sum_ref[at, main:] = last
         return carry
 
     lax.fori_loop(0, terms // together, term, 0)
@@ -246,6 +254,11 @@
     high, low = split(value)
     both = dot(jnp.concatenate([high, low], axis=0), table)
     return both[: value.shape[0]] + both[value.shape[0] :]
+
+
+def moved_tiles(value, table):
+    high, low = split(value)
+    return dot(jnp.concatenate([high, low], axis=1), jnp.concatenate([table, table], axis=0))
 
 
 def pack_kernel(count, source_ref, move_ref, a_ref, b_ref, loss_ref, out_ref, loss_out_ref, moves_ref, table_ref):
@@ -290,11 +303,17 @@
         return slice(at, at + len(self.parts[k]) * self.count)
 
 
+def two_rims(refs):
+    return (refs[0].at[0], refs[0].at[1]) if len(refs) == 1 else refs
+
+
 def first_kernel(
     count, rest, cells, cells_y,
     density_ref, below_ref, above_ref, kernel_ref, loss_ref, inverse_ref, forward_ref, rows_ref, speed_ref, moves_ref,
-    field_ref, up_ref, down_ref, modes_ref, sum_ref, rim_ref,
+    field_ref, *refs,
 ):
+    up_ref, down_ref = two_rims(refs[:-3])
+    modes_ref, sum_ref, rim_ref = refs[-3:]
     cells_x = density_ref.shape[0]
     middle = count // 2
     plane = count * count
@@ -318,7 +337,7 @@
     for k, part in enumerate(cells.parts):
         starts = [(x, y * plane // lanes * lanes) for x, y in part]
         values = jnp.concatenate([moved_on[x][:, at : at + 5 * lanes] for x, at in starts], axis=0)
-        field_ref[cells.part_rows(k)] = moved(values, moves_ref[k])
+        field_ref[cells.part_rows(k)] = moved_tiles(values, moves_ref[k])
     collide(field_ref, modes_ref, sum_ref, kernel_ref, loss_ref, inverse_ref, forward_ref, rows_ref, count, rest, 2)
     for x in range(cells_x):
         for k in range(2):
@@ -364,17 +383,17 @@
 
 def outer_kernel(
     count, rest, everything, inner, cells, cells_y,
-    given_ref, inner_ref, below_ref, above_ref, kernel_ref, loss_ref, inverse_ref, forward_ref, rows_ref, speed_ref,
-    moves_ref,
-    out_ref, field_ref, modes_ref, sum_ref,
+    given_ref, inner_ref, kernel_ref, loss_ref, inverse_ref, forward_ref, rows_ref, speed_ref, moves_ref, *refs,
 ):
+    below_ref, above_ref = two_rims(refs[:-4])
+    out_ref, field_ref, modes_ref, sum_ref = refs[-4:]
     plane = count * count
     sweep_y(given_ref, below_ref, above_ref, speed_ref, field_ref, everything, cells, cells_y, rest)
     collide(field_ref, modes_ref, sum_ref, kernel_ref, loss_ref, inverse_ref, forward_ref, rows_ref, count, rest, 2)
     pieces = {}
     for k in range(2):
         values = [field_ref[cells.part_rows(k)], inner_ref[inner.part_rows(k)]]
-        natural = moved(jnp.concatenate(values, axis=0), moves_ref[2 + k])
+        natural = moved_tiles(jnp.concatenate(values, axis=0), moves_ref[2 + k])
         for i, place in enumerate(cells.parts[k] + inner.parts[k]):
             pieces[place] = natural[i * count : (i + 1) * count]
     for x in range(out_ref.shape[0]):
@@ -457,17 +476,18 @@
         gains_b.reshape(-1, count),
         loss_rates.reshape(-1, count),
     )
-    rim_shape = jax.ShapeDtypeStruct((cells_x, 2, count, 3 * lanes), f32)
-    field, up, down = pl.pallas_call(
+    rim = (cells_x, 2, count, 3 * lanes)
+    mirrored = lax.axis_size("gy") == 2
+    rim_shapes = [jax.ShapeDtypeStruct((2, *rim), f32)] if mirrored else [jax.ShapeDtypeStruct(rim, f32)] * 2
+    field, *rims = pl.pallas_call(
         functools.partial(first_kernel, count, rest, everything, cells_y),
-        out_shape=(jax.ShapeDtypeStruct((everything.size, 5 * lanes), f32), rim_shape, rim_shape),
+        out_shape=(jax.ShapeDtypeStruct((everything.size, 5 * lanes), f32), *rim_shapes),
         scratch_shapes=scratch(everything) + [pltpu.VMEM((2, count, width), f32)],
         compiler_params=params(first_mib),
         cost_estimate=cost(everything),
         name="first",
     )(density, below, above, packed, packed_loss, *tables, row_speed, move_tables)
-    y_below = passed_along(up, "gy", 1)
-    y_above = passed_along(down, "gy", -1)
+    rims = [passed_along(value, "gy", steps) for value, steps in zip(rims, (1, -1))]
     inner_field = pl.pallas_call(
         functools.partial(inner_kernel, count, rest, everything, inner, cells_y),
         out_shape=jax.ShapeDtypeStruct((inner.size, 5 * lanes), f32),
@@ -483,7 +503,7 @@
         compiler_params=params(second_mib),
         cost_estimate=cost(outer),
         name="outer",
-    )(field, inner_field, y_below, y_above, packed, packed_loss, *tables, lane_speed, move_tables)
+    )(field, inner_field, packed, packed_loss, *tables, lane_speed, move_tables, *rims)
 
 
 def solution(mesh):

time: 45.5 us -> 45.1 us (level)
  waiting for transfers between devices: 0.83 us -> 1.4 us
  starting transfers between devices: 7.59 us -> 7.08 us
  Pallas kernels: 29.8 us -> 29.3 us
    ppermute x4 -> x3, waiting for transfers between devices: 0.83 us -> 1.4 us  [passed_along(): return lax.ppermute(value, axis, pairs)]
    ppermute x4 -> x3, starting transfers between devices: 7.59 us -> 7.08 us  [passed_along(): return lax.ppermute(value, axis, pairs)]
  transfers between devices with their start and end apart: 4 -> 3, of which waited for: 2 -> 2; matrix products, arithmetic and copies ran while one was open for 0% -> 0% of each run, Pallas kernels for 19% -> 19%
where the time goes in v3:
time: 45.1 us; the launch traced here: 44.8 us
  Pallas kernels  29.3 us (65%)
  starting transfers between devices  7.08 us (16%)
  local copies, waits for them, and re-layouts  6.91 us (15%)
  waiting for transfers between devices  1.4 us (3%)
    pallas_call x1, Pallas kernels, body(): pl.pallas_call(functools.partial(first_kernel, count, rest, everything, c...  11.6 us
    pallas_call x1, Pallas kernels, body(): pl.pallas_call(functools.partial(outer_kernel, count, rest, everything, i...  9.21 us
    ppermute x3, starting transfers between devices, passed_along(): return lax.ppermute(value, axis, pairs)  7.08 us
    unnamed x22, local copies, waits for them, and re-layouts  5.7 us
    pallas_call x1, Pallas kernels, body(): pl.pallas_call(functools.partial(inner_kernel, count, rest, everything, i...  4.33 us
    pallas_call x1, Pallas kernels, body(): pl.pallas_call(functools.partial(pack_kernel, count), grid=(steps,), in_s...  4.16 us
    ppermute x3, waiting for transfers between devices, passed_along(): return lax.ppermute(value, axis, pairs)  1.4 us
    slice x1, local copies, waits for them, and re-layouts, body(): above = passed_along(density[:2, :middle], 'gx', -1)  1.21 us
  transfers between devices with their start and end apart: 3, of which 2 were waited for; matrix products, arithmetic and copies ran while one was open for 0% of the time, Pallas kernels for 19%

profile of v3, /device:TPU:0, one launch (start us, length us, event | category | flops | bytes accessed | tf_op | source)
XLA Modules:
  0.0 44.8 jit_solution(15064636043841087243)
XLA Ops:
  0.0 1.2 %fusion = (f32[2,12,3456]{2,1,0:T(8,128)S(1)}, f32[2,12,3456]{2,1,0:T(8,128)S(1)}) fusion(f32[2,24,3456]{2,1,0:T(8,128)} %density_ref.1), kind=kLoop, calls=%fused_computation | loop fusion | bytes 1327104 | tf_op jit(solution)/shard_map/slice | solution.py:444
  1.2 5.5 %collective-permute-start.1 = (f32[2,12,3456]{2,1,0:T(8,128)S(1)}, f32[2,12,3456]{2,1,0:T(8,128)S(1)}, u32[]{:S(2)}, u32[]{:S(2)}) collective-permute-start(f32[2,12,3456]{2,1,0:T(8,128)S(1)} %get-tuple-element.15), channel_id=1, source_target_pairs={{0,30},{2,0},{4,2},{6,4},{8,6},{10,8},{12,10},{14,12},{16,14},{18,... | collective-permute-start | bytes 995336 | tf_op jit(solution)/shard_map/ppermute | solution.py:23
  6.7 0.0 collective-permute-start
  6.7 0.0 copy-start.1
  6.7 1.7 %copy-done.1 = f32[8,24,24,24]{3,2,1,0:T(8,128)S(1)} copy-done((f32[8,24,24,24]{3,2,1,0:T(8,128)S(1)}, f32[8,24,24,24]{3,2,1,0:T(8,128)}, u32[]{:S(2)}) %copy-start.1) | copy-done | bytes 442392
  8.4 0.0 copy-start.2
  8.4 1.7 %copy-done.2 = f32[8,24,24,24]{3,2,1,0:T(8,128)S(1)} copy-done((f32[8,24,24,24]{3,2,1,0:T(8,128)S(1)}, f32[8,24,24,24]{3,2,1,0:T(8,128)}, u32[]{:S(2)}) %copy-start.2) | copy-done | bytes 442392
  10.0 1.0 %copy-done.3 = f32[24,24,24]{2,1,0:T(8,128)S(1)} copy-done((f32[24,24,24]{2,1,0:T(8,128)S(1)}, f32[24,24,24]{2,1,0:T(8,128)}, u32[]{:S(2)}) %copy-start.3) | copy-done | bytes 55320
  11.0 0.0 copy-start.9
  11.0 0.7 %copy-done.9 = s32[4,1,640]{2,1,0:T(1,128)S(1)} copy-done((s32[4,1,640]{2,1,0:T(1,128)S(1)}, s32[4,1,640]{2,1,0:T(1,128)}, u32[]{:S(2)}) %copy-start.9) | copy-done | bytes 10264
  11.7 0.0 copy-start.10
  11.7 0.7 %copy-done.10 = s32[1,768]{1,0:T(1,128)S(1)} copy-done((s32[1,768]{1,0:T(1,128)S(1)}, s32[1,768]{1,0:T(1,128)}, u32[]{:S(2)}) %copy-start.10) | copy-done | bytes 3096
  12.4 0.0 copy-start
  12.4 0.0 copy-start.4
  12.4 0.0 copy-start.5
  12.4 0.0 copy-start.6
  12.4 0.0 copy-start.7
  12.4 4.2 %pack.1 = (f32[8,2,24,768]{3,2,1,0:T(8,128)S(1)}, f32[24,768]{1,0:T(8,128)S(1)}, bf16[4,640,640]{2,1,0:T(8,128)(2,1)S(1)}) custom-call(s32[1,768]{1,0:T(1,128)S(1)} %copy-done.10, s32[4,1,640]{2,1,0:T(1,128)S(1)} %copy-done.9, f32[4608,24]{1,0:T(8,128)S(1)} %bitcast.3, f32[4608,24]{1,0:T(8,128)S(1)} %bitcast.4, f32[576,24]{1,0:T(8,128)S(1)} %bitcast.5), custom_call_target="tpu_custom_call" | custom-call | flops 4294967296 | bytes 8388608 | tf_op jit(solution)/shard_map/pack/pallas_call | solution.py:448
  16.6 0.0 collective-permute-done.1.above_ref
  16.6 0.5 %collective-permute-done.below_ref = f32[2,12,3456]{2,1,0:T(8,128)S(1)} collective-permute-done((f32[2,12,3456]{2,1,0:T(8,128)S(1)}, f32[2,12,3456]{2,1,0:T(8,128)S(1)}, u32[]{:S(2)}, u32[]{:S(2)}) %collective-permute-start) | collective-permute-done | bytes 331808 | tf_op jit(solution)/shard_map/ppermute | solution.py:23
  17.1 0.0 copy-done
  17.1 0.0 copy-done.4
  17.1 0.0 copy-done.5
  17.1 0.0 copy-done.6
  17.2 0.0 copy-done.7
  17.2 0.0 copy-start.8
  17.2 11.6 %first.1 = (f32[288,640]{1,0:T(8,128)S(1)}, f32[2,2,2,24,384]{4,3,2,1,0:T(8,128)S(1)}) custom-call(f32[2,24,3456]{2,1,0:T(8,128)S(1)} %copy-done, f32[2,12,3456]{2,1,0:T(8,128)S(1)} %collective-permute-done.below_ref, f32[2,12,3456]{2,1,0:T(8,128)S(1)} %collective-permute-done.1.above_ref, f32[8,2,24,768]{3,2,1,0:T(8,128)S(1)} %get-tuple-element.10.kernel_ref, ...), custom_call_target="tpu_custom_call" | custom-call | flops 38654705664 | bytes 4194304 | tf_op jit(solution)/shard_map/first/pallas_call | solution.py:482
  28.8 1.6 %collective-permute-start.2 = (f32[2,2,2,24,384]{4,3,2,1,0:T(8,128)S(1)}, f32[2,2,2,24,384]{4,3,2,1,0:T(8,128)S(1)}, u32[]{:S(2)}, u32[]{:S(2)}) collective-permute-start(f32[2,2,2,24,384]{4,3,2,1,0:T(8,128)S(1)} %get-tuple-element.14), channel_id=1, source_target_pairs={{0,1},{1,0},{2,3},{3,2},{4,5},{5,4},{6,7},{7,6},{8,9},{9,8},{10,11... | collective-permute-start | bytes 884744 | tf_op jit(solution)/shard_map/ppermute | solution.py:23
  30.4 0.0 copy-done.8
  30.4 4.3 %inner.1.inner_ref = f32[96,640]{1,0:T(8,128)S(1)} custom-call(f32[288,640]{1,0:T(8,128)S(1)} %get-tuple-element.13.given_ref, f32[8,2,24,768]{3,2,1,0:T(8,128)S(1)} %get-tuple-element.10.kernel_ref, f32[24,768]{1,0:T(8,128)S(1)} %get-tuple-element.11.loss_ref, bf16[4,512,256]{2,1,0:T(8,128)(2,1)S(1)} %copy-done.5, bf16[4,640,256]{2,1,0:T(8,128)(2,1)S(1)} %copy-done.4, ...), custom_call_target="tpu_custom_call" | custom-call | flops 12884901888 | bytes 4194304 | tf_op jit(solution)/shard_map/inner/pallas_call | solution.py:491
  34.7 0.9 %collective-permute-done.2.refs_0_ = f32[2,2,2,24,384]{4,3,2,1,0:T(8,128)S(1)} collective-permute-done((f32[2,2,2,24,384]{4,3,2,1,0:T(8,128)S(1)}, f32[2,2,2,24,384]{4,3,2,1,0:T(8,128)S(1)}, u32[]{:S(2)}, u32[]{:S(2)}) %collective-permute-start.2) | collective-permute-done | bytes 294944 | tf_op jit(solution)/shard_map/ppermute | solution.py:23
  35.6 9.2 %outer.1 = f32[2,24,3456]{2,1,0:T(8,128)} custom-call(f32[288,640]{1,0:T(8,128)S(1)} %get-tuple-element.13.given_ref, f32[96,640]{1,0:T(8,128)S(1)} %inner.1.inner_ref, f32[8,2,24,768]{3,2,1,0:T(8,128)S(1)} %get-tuple-element.10.kernel_ref, f32[24,768]{1,0:T(8,128)S(1)} %get-tuple-element.11.loss_ref, bf16[4,512,256]{2,1,0:T(8,128)(2,1)S(1)} %copy-done.5, ...), custom_call_target="tpu_custom_call" | custom-call | flops 25769803776 | bytes 4194304 | tf_op jit(solution)/shard_map/outer/pallas_call | solution.py:499
  (1 shorter events, 0.0 us)
Async XLA Ops:
  1.2 15.4 %collective-permute-start.1 = (f32[2,12,3456]{2,1,0:T(8,128)S(1)}, f32[2,12,3456]{2,1,0:T(8,128)S(1)}, u32[]{:S(2)}, u32[]{:S(2)}) collective-permute-start(f32[2,12,3456]{2,1,0:T(8,128)S(1)} %get-tuple-element.15), channel_id=1, source_target_pairs={{0,30},{2,0},{4,2},{6,4},{8,6},{10,8},{12,10},{14,12},{16,14},{18,... | collective-permute-start | bytes 995336 | tf_op jit(solution)/shard_map/ppermute | solution.py:23
  6.7 10.4 %collective-permute-start = (f32[2,12,3456]{2,1,0:T(8,128)S(1)}, f32[2,12,3456]{2,1,0:T(8,128)S(1)}, u32[]{:S(2)}, u32[]{:S(2)}) collective-permute-start(f32[2,12,3456]{2,1,0:T(8,128)S(1)} %get-tuple-element.16), channel_id=1, source_target_pairs={{0,2},{2,4},{4,6},{6,8},{8,10},{10,12},{12,14},{14,16},{16,18},{18... | collective-permute-start | bytes 995336 | tf_op jit(solution)/shard_map/ppermute | solution.py:23
  6.7 1.7 %copy-start.1 = (f32[8,24,24,24]{3,2,1,0:T(8,128)S(1)}, f32[8,24,24,24]{3,2,1,0:T(8,128)}, u32[]{:S(2)}) copy-start(f32[8,24,24,24]{3,2,1,0:T(8,128)} %param.12) | copy-start | bytes 1327108
  8.4 1.7 %copy-start.2 = (f32[8,24,24,24]{3,2,1,0:T(8,128)S(1)}, f32[8,24,24,24]{3,2,1,0:T(8,128)}, u32[]{:S(2)}) copy-start(f32[8,24,24,24]{3,2,1,0:T(8,128)} %param.13) | copy-start | bytes 1327108
  10.0 1.0 %copy-start.3 = (f32[24,24,24]{2,1,0:T(8,128)S(1)}, f32[24,24,24]{2,1,0:T(8,128)}, u32[]{:S(2)}) copy-start(f32[24,24,24]{2,1,0:T(8,128)} %param.14) | copy-start | bytes 165892
  11.0 0.7 %copy-start.9 = (s32[4,1,640]{2,1,0:T(1,128)S(1)}, s32[4,1,640]{2,1,0:T(1,128)}, u32[]{:S(2)}) copy-start(s32[4,1,640]{2,1,0:T(1,128)} %constant.20.clone.move_ref) | copy-start | bytes 30724
  11.7 0.7 %copy-start.10 = (s32[1,768]{1,0:T(1,128)S(1)}, s32[1,768]{1,0:T(1,128)}, u32[]{:S(2)}) copy-start(s32[1,768]{1,0:T(1,128)} %constant.19.clone.source_ref) | copy-start | bytes 9220
  12.4 4.7 %copy-start = (f32[2,24,3456]{2,1,0:T(8,128)S(1)}, f32[2,24,3456]{2,1,0:T(8,128)}, u32[]{:S(2)}) copy-start(f32[2,24,3456]{2,1,0:T(8,128)} %density_ref.1) | copy-start | bytes 1990660
  12.4 4.7 %copy-start.4 = (bf16[4,640,256]{2,1,0:T(8,128)(2,1)S(1)}, bf16[4,640,256]{2,1,0:T(8,128)(2,1)}, u32[]{:S(2)}) copy-start(bf16[4,640,256]{2,1,0:T(8,128)(2,1)} %constant.17.clone.forward_ref) | copy-start | bytes 3932164
  12.4 4.7 %copy-start.5 = (bf16[4,512,256]{2,1,0:T(8,128)(2,1)S(1)}, bf16[4,512,256]{2,1,0:T(8,128)(2,1)}, u32[]{:S(2)}) copy-start(bf16[4,512,256]{2,1,0:T(8,128)(2,1)} %constant.16.clone.inverse_ref) | copy-start | bytes 3145732
  12.4 4.7 %copy-start.6 = (bf16[2,192,192]{2,1,0:T(8,128)(2,1)S(1)}, bf16[2,192,192]{2,1,0:T(8,128)(2,1)}, u32[]{:S(2)}) copy-start(bf16[2,192,192]{2,1,0:T(8,128)(2,1)} %constant.18.clone.rows_ref) | copy-start | bytes 442372
  12.4 4.8 %copy-start.7 = (f32[24,3]{1,0:T(8,128)S(1)}, f32[24,3]{1,0:T(8,128)}, u32[]{:S(2)}) copy-start(f32[24,3]{1,0:T(8,128)} %constant.15.clone.speed_ref) | copy-start | bytes 868
  17.2 13.2 %copy-start.8 = (f32[3,640]{1,0:T(4,128)S(1)}, f32[3,640]{1,0:T(4,128)}, u32[]{:S(2)}) copy-start(f32[3,640]{1,0:T(4,128)} %constant.14.clone.speed_ref) | copy-start | bytes 23044
  28.8 6.8 %collective-permute-start.2 = (f32[2,2,2,24,384]{4,3,2,1,0:T(8,128)S(1)}, f32[2,2,2,24,384]{4,3,2,1,0:T(8,128)S(1)}, u32[]{:S(2)}, u32[]{:S(2)}) collective-permute-start(f32[2,2,2,24,384]{4,3,2,1,0:T(8,128)S(1)} %get-tuple-element.14), channel_id=1, source_target_pairs={{0,1},{1,0},{2,3},{3,2},{4,5},{5,4},{6,7},{7,6},{8,9},{9,8},{10,11... | collective-permute-start | bytes 884744 | tf_op jit(solution)/shard_map/ppermute | solution.py:23

commit v4 on v3

--- a/solution.py
+++ b/solution.py
@@ -21,6 +21,11 @@
     count = lax.axis_size(axis)
     pairs = [(source, (source + steps) % count) for source in range(count)]
     return lax.ppermute(value, axis, pairs)
+
+
+def passed_along_line(value, axis, steps):
+    count = lax.axis_size(axis)
+    return lax.ppermute(value, axis, [(k, k + steps) for k in range(count) if 0 <= k + steps < count])
 
 
 def cosine_table(count):
@@ -309,7 +314,8 @@
 
 def first_kernel(
     count, rest, cells, cells_y,
-    density_ref, below_ref, above_ref, kernel_ref, loss_ref, inverse_ref, forward_ref, rows_ref, speed_ref, moves_ref,
+    density_ref, below_ref, above_ref, closing_ref, is_end_ref,
+    kernel_ref, loss_ref, inverse_ref, forward_ref, rows_ref, speed_ref, moves_ref,
     field_ref, *refs,
 ):
     up_ref, down_ref = two_rims(refs[:-3])
@@ -320,6 +326,17 @@
     for i in range(2):
         rim_ref[i, :middle] = above_ref[i]
         rim_ref[i, middle:] = below_ref[i]
+
+    @pl.when(is_end_ref[0] == 1)
+    def _():
+        for i in range(2):
+            rim_ref[i, :middle] = closing_ref[i]
+
+    @pl.when(is_end_ref[1] == 1)
+    def _():
+        for i in range(2):
+            rim_ref[i, middle:] = closing_ref[i]
+
     positive = lax.broadcasted_iota(jnp.int32, (count, 1), 0) >= middle
 
     def behind(x):
@@ -431,6 +448,8 @@
     group = min(cells_together(c.size // count) for c in (everything, inner, outer))
     tables = [jnp.asarray(t) for t in (inverse_tables(count), forward_tables(count), row_tables(count, group))]
 
+    whole = pl.BlockSpec(memory_space=pltpu.VMEM)
+
     def params(mib):
         return pltpu.CompilerParams(vmem_limit_bytes=mib << 20)
 
@@ -440,8 +459,15 @@
     def cost(cells):
         return pl.CostEstimate(flops=cells.size << 27, bytes_accessed=4 << 20, transcendentals=0)
 
-    below = passed_along(density[-2:, middle:], "gx", 1)
-    above = passed_along(density[:2, :middle], "gx", -1)
+    place = lax.axis_index("gx")
+    ends = lax.axis_size("gx")
+    leaving_up, leaving_down = density[-2:, middle:], density[:2, :middle]
+    closing = lax.ppermute(
+        jnp.where(place == 0, leaving_down, leaving_up), "gx", [(0, ends - 1), (ends - 1, 0)]
+    )
+    below = passed_along_line(leaving_up, "gx", 1)
+    above = passed_along_line(leaving_down, "gx", -1)
+    is_end = jnp.stack([place == ends - 1, place == 0]).astype(jnp.int32)
     steps = 2 if terms % 2 == 0 else 1
     taken = terms // steps
     gain_spec = pl.BlockSpec((taken * plane, count), lambda i: (i, 0))
@@ -472,21 +498,22 @@
     )(
         jnp.asarray(mode_lanes(count)[None]),
         jnp.asarray(moves),
-        gains_a.reshape(-1, count),
-        gains_b.reshape(-1, count),
-        loss_rates.reshape(-1, count),
+        pltpu.with_memory_space_constraint(gains_a.reshape(-1, count), pltpu.HBM),
+        pltpu.with_memory_space_constraint(gains_b.reshape(-1, count), pltpu.HBM),
+        pltpu.with_memory_space_constraint(loss_rates.reshape(-1, count), pltpu.HBM),
     )
     rim = (cells_x, 2, count, 3 * lanes)
     mirrored = lax.axis_size("gy") == 2
     rim_shapes = [jax.ShapeDtypeStruct((2, *rim), f32)] if mirrored else [jax.ShapeDtypeStruct(rim, f32)] * 2
     field, *rims = pl.pallas_call(
         functools.partial(first_kernel, count, rest, everything, cells_y),
+        in_specs=[whole] * 4 + [pl.BlockSpec(memory_space=pltpu.SMEM)] + [whole] * 7,
         out_shape=(jax.ShapeDtypeStruct((everything.size, 5 * lanes), f32), *rim_shapes),
         scratch_shapes=scratch(everything) + [pltpu.VMEM((2, count, width), f32)],
         compiler_params=params(first_mib),
         cost_estimate=cost(everything),
         name="first",
-    )(density, below, above, packed, packed_loss, *tables, row_speed, move_tables)
+    )(density, below, above, closing, is_end, packed, packed_loss, *tables, row_speed, move_tables)
     rims = [passed_along(value, "gy", steps) for value, steps in zip(rims, (1, -1))]
     inner_field = pl.pallas_call(
         functools.partial(inner_kernel, count, rest, everything, inner, cells_y),

time: 45.1 us -> 50.9 us (1.13)
  local copies, waits for them, and re-layouts: 6.91 us -> 1.41 us
  starting transfers between devices: 7.08 us -> 11.5 us
  Pallas kernels: 29.3 us -> 32.3 us
  waiting for transfers between devices: 1.4 us -> 3.85 us
  other arithmetic: 0 us -> 1.31 us
    ppermute x0 -> x3, starting transfers between devices: none -> 9.96 us  [the longest x1 7.35 us: body(): lax.ppermute(jnp.where(place == 0, leaving_down, leaving_up), 'gx', [(0,...]
    ppermute x3 -> x1, starting transfers between devices: 7.08 us -> 1.58 us  [passed_along(): return lax.ppermute(value, axis, pairs)]
    unnamed x22 -> x16, local copies, waits for them, and re-layouts: 5.7 us -> 1.41 us
    ppermute x3 -> x1, waiting for transfers between devices: 1.4 us -> 3.84 us  [passed_along(): return lax.ppermute(value, axis, pairs)]
    pallas_call x1, Pallas kernels: 4.16 us -> 6.01 us  [body(): pl.pallas_call(functools.partial(pack_kernel, count), grid=(steps,), in_s...]
    select_n x0 -> x1, other arithmetic: none -> 1.23 us  [body(): jnp.where(place == 0, leaving_down, leaving_up)]
    slice x1 -> x0, local copies, waits for them, and re-layouts: 1.21 us -> none  [body(): above = passed_along(density[:2, :middle], 'gx', -1)]
    pallas_call x1, Pallas kernels: 11.6 us -> 12.6 us  [body(): pl.pallas_call(functools.partial(first_kernel, count, rest, everything, c...]
  transfers between devices with their start and end apart: 3 -> 4, of which waited for: 2 -> 1; matrix products, arithmetic and copies ran while one was open for 0% -> 0% of each run, Pallas kernels for 19% -> 21%
where the time goes in v4:
time: 50.9 us; the launch traced here: 50.6 us
  Pallas kernels  32.3 us (63%)
  starting transfers between devices  11.5 us (23%)
  waiting for transfers between devices  3.85 us (8%)
  local copies, waits for them, and re-layouts  1.41 us (3%)
  other arithmetic  1.31 us (3%)
    pallas_call x1, Pallas kernels, body(): pl.pallas_call(functools.partial(first_kernel, count, rest, everything, c...  12.6 us
    pallas_call x1, Pallas kernels, body(): pl.pallas_call(functools.partial(outer_kernel, count, rest, everything, i...  9.33 us
    ppermute x1, starting transfers between devices, body(): lax.ppermute(jnp.where(place == 0, leaving_down, leaving_up), 'gx', [(0,...  7.35 us
    pallas_call x1, Pallas kernels, body(): pl.pallas_call(functools.partial(pack_kernel, count), grid=(steps,), in_s...  6.01 us
    pallas_call x1, Pallas kernels, body(): pl.pallas_call(functools.partial(inner_kernel, count, rest, everything, i...  4.4 us
    ppermute x1, waiting for transfers between devices, passed_along(): return lax.ppermute(value, axis, pairs)  3.84 us
    ppermute x2, starting transfers between devices, passed_along_line(): lax.ppermute(value, axis, [(k, k + steps) for k in range(count) if 0 <= k...  2.61 us
    ppermute x1, starting transfers between devices, passed_along(): return lax.ppermute(value, axis, pairs)  1.58 us
  transfers between devices with their start and end apart: 4, of which 1 were waited for; matrix products, arithmetic and copies ran while one was open for 0% of the time, Pallas kernels for 21%

profile of v4, /device:TPU:0, one launch (start us, length us, event | category | flops | bytes accessed | tf_op | source)
XLA Modules:
  0.0 50.6 jit_solution(12687922090413488961)
XLA Ops:
  0.0 1.2 %broadcast_select_fusion = (f32[2,12,3456]{2,1,0:T(8,128)S(1)}, f32[2,12,3456]{2,1,0:T(8,128)S(1)}, f32[2,12,3456]{2,1,0:T(8,128)S(1)}) fusion(pred[]{:T(512)} %eq.7, f32[2,24,3456]{2,1,0:T(8,128)} %density_ref.1), kind=kLoop, calls=%fused_computation | loop fusion | flops 82944 | bytes 1658881 | tf_op jit(solution)/shard_map/jit(_where)/select_n | solution.py:466
  1.2 7.4 %collective-permute-start.2 = (f32[2,12,3456]{2,1,0:T(8,128)S(1)}, f32[2,12,3456]{2,1,0:T(8,128)S(1)}, u32[]{:S(2)}, u32[]{:S(2)}) collective-permute-start(f32[2,12,3456]{2,1,0:T(8,128)S(1)} %get-tuple-element.15), channel_id=1, source_target_pairs={{0,30},{30,0},{1,31},{31,1}} | collective-permute-start | bytes 995336 | tf_op jit(solution)/shard_map/ppermute | solution.py:465
  8.6 1.3 %collective-permute-start = (f32[2,12,3456]{2,1,0:T(8,128)S(1)}, f32[2,12,3456]{2,1,0:T(8,128)S(1)}, u32[]{:S(2)}, u32[]{:S(2)}) collective-permute-start(f32[2,12,3456]{2,1,0:T(8,128)S(1)} %get-tuple-element.16), channel_id=1, source_target_pairs={{0,2},{2,4},{4,6},{6,8},{8,10},{10,12},{12,14},{14,16},{16,18},{18... | collective-permute-start | bytes 995336 | tf_op jit(solution)/shard_map/ppermute | solution.py:28
  9.9 1.3 %collective-permute-start.1 = (f32[2,12,3456]{2,1,0:T(8,128)S(1)}, f32[2,12,3456]{2,1,0:T(8,128)S(1)}, u32[]{:S(2)}, u32[]{:S(2)}) collective-permute-start(f32[2,12,3456]{2,1,0:T(8,128)S(1)} %get-tuple-element.17), channel_id=1, source_target_pairs={{2,0},{4,2},{6,4},{8,6},{10,8},{12,10},{14,12},{16,14},{18,16},{20... | collective-permute-start | bytes 995336 | tf_op jit(solution)/shard_map/ppermute | solution.py:28
  11.2 0.1 add_convert_fusion.is_end_ref
  11.3 0.0 copy-start.6
  11.3 0.7 %copy-done.6 = s32[4,1,640]{2,1,0:T(1,128)S(1)} copy-done((s32[4,1,640]{2,1,0:T(1,128)S(1)}, s32[4,1,640]{2,1,0:T(1,128)}, u32[]{:S(2)}) %copy-start.6) | copy-done | bytes 10264
  12.0 0.0 copy-start.7
  12.0 0.7 %copy-done.7 = s32[1,768]{1,0:T(1,128)S(1)} copy-done((s32[1,768]{1,0:T(1,128)S(1)}, s32[1,768]{1,0:T(1,128)}, u32[]{:S(2)}) %copy-start.7) | copy-done | bytes 3096
  12.7 0.0 copy-start
  12.7 0.0 copy-start.1
  12.7 0.0 copy-start.2
  12.7 0.0 copy-start.3
  12.7 0.0 copy-start.4
  12.7 6.0 %pack.1 = (f32[8,2,24,768]{3,2,1,0:T(8,128)S(1)}, f32[24,768]{1,0:T(8,128)S(1)}, bf16[4,640,640]{2,1,0:T(8,128)(2,1)S(1)}) custom-call(s32[1,768]{1,0:T(1,128)S(1)} %copy-done.7, s32[4,1,640]{2,1,0:T(1,128)S(1)} %copy-done.6, f32[4608,24]{1,0:T(8,128)} %bitcast.5, f32[4608,24]{1,0:T(8,128)} %bitcast.6, f32[576,24]{1,0:T(8,128)} %bitcast.7), custom_call_target="tpu_custom_call" | custom-call | flops 4294967296 | bytes 8388608 | tf_op jit(solution)/shard_map/pack/pallas_call | solution.py:474
  18.7 0.0 collective-permute-done.2.closing_ref
  18.7 0.0 collective-permute-done.below_ref
  18.8 0.0 collective-permute-done.1.above_ref
  18.8 0.0 copy-done
  18.8 0.0 copy-done.1
  18.8 0.0 copy-done.2
  18.8 0.0 copy-done.3
  18.8 0.0 copy-done.4
  18.8 0.0 copy-start.5
  18.8 12.6 %first.1 = (f32[288,640]{1,0:T(8,128)S(1)}, f32[2,2,2,24,384]{4,3,2,1,0:T(8,128)S(1)}) custom-call(f32[2,24,3456]{2,1,0:T(8,128)S(1)} %copy-done, f32[2,12,3456]{2,1,0:T(8,128)S(1)} %collective-permute-done.below_ref, f32[2,12,3456]{2,1,0:T(8,128)S(1)} %collective-permute-done.1.above_ref, f32[2,12,3456]{2,1,0:T(8,128)S(1)} %collective-permute-done.2.closing_ref, ...), custom_call_target="tpu_custom_call" | custom-call | flops 38654705664 | bytes 4194304 | tf_op jit(solution)/shard_map/first/pallas_call | solution.py:508
  31.4 1.6 %collective-permute-start.3 = (f32[2,2,2,24,384]{4,3,2,1,0:T(8,128)S(1)}, f32[2,2,2,24,384]{4,3,2,1,0:T(8,128)S(1)}, u32[]{:S(2)}, u32[]{:S(2)}) collective-permute-start(f32[2,2,2,24,384]{4,3,2,1,0:T(8,128)S(1)} %get-tuple-element.14), channel_id=1, source_target_pairs={{0,1},{1,0},{2,3},{3,2},{4,5},{5,4},{6,7},{7,6},{8,9},{9,8},{10,11... | collective-permute-start | bytes 884744 | tf_op jit(solution)/shard_map/ppermute | solution.py:23
  33.0 0.0 copy-done.5
  33.0 4.4 %inner.1.inner_ref = f32[96,640]{1,0:T(8,128)S(1)} custom-call(f32[288,640]{1,0:T(8,128)S(1)} %get-tuple-element.13.given_ref, f32[8,2,24,768]{3,2,1,0:T(8,128)S(1)} %get-tuple-element.10.kernel_ref, f32[24,768]{1,0:T(8,128)S(1)} %get-tuple-element.11.loss_ref, bf16[4,512,256]{2,1,0:T(8,128)(2,1)S(1)} %copy-done.2, bf16[4,640,256]{2,1,0:T(8,128)(2,1)S(1)} %copy-done.1, ...), custom_call_target="tpu_custom_call" | custom-call | flops 12884901888 | bytes 4194304 | tf_op jit(solution)/shard_map/inner/pallas_call | solution.py:518
  37.4 3.8 %collective-permute-done.3.refs_0_ = f32[2,2,2,24,384]{4,3,2,1,0:T(8,128)S(1)} collective-permute-done((f32[2,2,2,24,384]{4,3,2,1,0:T(8,128)S(1)}, f32[2,2,2,24,384]{4,3,2,1,0:T(8,128)S(1)}, u32[]{:S(2)}, u32[]{:S(2)}) %collective-permute-start.3) | collective-permute-done | bytes 294944 | tf_op jit(solution)/shard_map/ppermute | solution.py:23
  41.3 9.3 %outer.1 = f32[2,24,3456]{2,1,0:T(8,128)} custom-call(f32[288,640]{1,0:T(8,128)S(1)} %get-tuple-element.13.given_ref, f32[96,640]{1,0:T(8,128)S(1)} %inner.1.inner_ref, f32[8,2,24,768]{3,2,1,0:T(8,128)S(1)} %get-tuple-element.10.kernel_ref, f32[24,768]{1,0:T(8,128)S(1)} %get-tuple-element.11.loss_ref, bf16[4,512,256]{2,1,0:T(8,128)(2,1)S(1)} %copy-done.2, ...), custom_call_target="tpu_custom_call" | custom-call | flops 25769803776 | bytes 4194304 | tf_op jit(solution)/shard_map/outer/pallas_call | solution.py:526
Async XLA Ops:
  1.2 17.5 %collective-permute-start.2 = (f32[2,12,3456]{2,1,0:T(8,128)S(1)}, f32[2,12,3456]{2,1,0:T(8,128)S(1)}, u32[]{:S(2)}, u32[]{:S(2)}) collective-permute-start(f32[2,12,3456]{2,1,0:T(8,128)S(1)} %get-tuple-element.15), channel_id=1, source_target_pairs={{0,30},{30,0},{1,31},{31,1}} | collective-permute-start | bytes 995336 | tf_op jit(solution)/shard_map/ppermute | solution.py:465
  8.6 10.2 %collective-permute-start = (f32[2,12,3456]{2,1,0:T(8,128)S(1)}, f32[2,12,3456]{2,1,0:T(8,128)S(1)}, u32[]{:S(2)}, u32[]{:S(2)}) collective-permute-start(f32[2,12,3456]{2,1,0:T(8,128)S(1)} %get-tuple-element.16), channel_id=1, source_target_pairs={{0,2},{2,4},{4,6},{6,8},{8,10},{10,12},{12,14},{14,16},{16,18},{18... | collective-permute-start | bytes 995336 | tf_op jit(solution)/shard_map/ppermute | solution.py:28
  9.9 8.8 %collective-permute-start.1 = (f32[2,12,3456]{2,1,0:T(8,128)S(1)}, f32[2,12,3456]{2,1,0:T(8,128)S(1)}, u32[]{:S(2)}, u32[]{:S(2)}) collective-permute-start(f32[2,12,3456]{2,1,0:T(8,128)S(1)} %get-tuple-element.17), channel_id=1, source_target_pairs={{2,0},{4,2},{6,4},{8,6},{10,8},{12,10},{14,12},{16,14},{18,16},{20... | collective-permute-start | bytes 995336 | tf_op jit(solution)/shard_map/ppermute | solution.py:28
  11.3 0.7 %copy-start.6 = (s32[4,1,640]{2,1,0:T(1,128)S(1)}, s32[4,1,640]{2,1,0:T(1,128)}, u32[]{:S(2)}) copy-start(s32[4,1,640]{2,1,0:T(1,128)} %constant.30.clone.move_ref) | copy-start | bytes 30724
  12.0 0.7 %copy-start.7 = (s32[1,768]{1,0:T(1,128)S(1)}, s32[1,768]{1,0:T(1,128)}, u32[]{:S(2)}) copy-start(s32[1,768]{1,0:T(1,128)} %constant.29.clone.source_ref) | copy-start | bytes 9220
  12.7 6.1 %copy-start = (f32[2,24,3456]{2,1,0:T(8,128)S(1)}, f32[2,24,3456]{2,1,0:T(8,128)}, u32[]{:S(2)}) copy-start(f32[2,24,3456]{2,1,0:T(8,128)} %density_ref.1) | copy-start | bytes 1990660
  12.7 6.1 %copy-start.1 = (bf16[4,640,256]{2,1,0:T(8,128)(2,1)S(1)}, bf16[4,640,256]{2,1,0:T(8,128)(2,1)}, u32[]{:S(2)}) copy-start(bf16[4,640,256]{2,1,0:T(8,128)(2,1)} %constant.27.clone.forward_ref) | copy-start | bytes 3932164
  12.7 6.1 %copy-start.2 = (bf16[4,512,256]{2,1,0:T(8,128)(2,1)S(1)}, bf16[4,512,256]{2,1,0:T(8,128)(2,1)}, u32[]{:S(2)}) copy-start(bf16[4,512,256]{2,1,0:T(8,128)(2,1)} %constant.26.clone.inverse_ref) | copy-start | bytes 3145732
  12.7 6.1 %copy-start.3 = (bf16[2,192,192]{2,1,0:T(8,128)(2,1)S(1)}, bf16[2,192,192]{2,1,0:T(8,128)(2,1)}, u32[]{:S(2)}) copy-start(bf16[2,192,192]{2,1,0:T(8,128)(2,1)} %constant.28.clone.rows_ref) | copy-start | bytes 442372
  12.7 6.1 %copy-start.4 = (f32[24,3]{1,0:T(8,128)S(1)}, f32[24,3]{1,0:T(8,128)}, u32[]{:S(2)}) copy-start(f32[24,3]{1,0:T(8,128)} %constant.25.clone.speed_ref) | copy-start | bytes 868
  18.8 14.2 %copy-start.5 = (f32[3,640]{1,0:T(4,128)S(1)}, f32[3,640]{1,0:T(4,128)}, u32[]{:S(2)}) copy-start(f32[3,640]{1,0:T(4,128)} %constant.24.clone.speed_ref) | copy-start | bytes 23044
  31.4 9.8 %collective-permute-start.3 = (f32[2,2,2,24,384]{4,3,2,1,0:T(8,128)S(1)}, f32[2,2,2,24,384]{4,3,2,1,0:T(8,128)S(1)}, u32[]{:S(2)}, u32[]{:S(2)}) collective-permute-start(f32[2,2,2,24,384]{4,3,2,1,0:T(8,128)S(1)} %get-tuple-element.14), channel_id=1, source_target_pairs={{0,1},{1,0},{2,3},{3,2},{4,5},{5,4},{6,7},{7,6},{8,9},{9,8},{10,11... | collective-permute-start | bytes 884744 | tf_op jit(solution)/shard_map/ppermute | solution.py:23

commit v5 on v3

--- a/solution.py
+++ b/solution.py
@@ -7,6 +7,7 @@
 from jax.experimental import pallas as pl
 from jax.experimental.pallas import tpu as pltpu
 from jax.sharding import PartitionSpec as P
+
 
 courant_max = 1.6
 collide_step = 0.2
@@ -201,10 +202,10 @@
     return jnp.concatenate(list(main) + [last], axis=1)
 
 
-def collide(field_ref, modes_ref, sum_ref, kernel_ref, loss_ref, inverse_ref, forward_ref, rows_ref, count, rest, most):
+def collide(field_ref, modes_ref, sum_ref, a_ref, b_ref, loss_ref, inverse_ref, forward_ref, rows_ref, count, rest, most):
     rows = field_ref.shape[0]
     cells = rows // count
-    terms = kernel_ref.shape[0]
+    terms = a_ref.shape[0]
     together = max(n for n in range(1, most + 1) if terms % n == 0)
     main = 4 * lanes
     size = rows_ref.shape[2] // 2
@@ -221,7 +222,7 @@
         sum_ref[at] = -field_ref[at] * part
 
     def term(step, carry):
-        factors = [kernel_ref[together * step + k, side] for k in range(together) for side in range(2)]
+        factors = [ref[together * step + k] for k in range(together) for ref in (a_ref, b_ref)]
         plane = inverse_plane(jnp.concatenate([scaled(f) for f in factors], axis=0), inverse_ref, rest)
         pairs = []
         for k in range(together):
@@ -261,27 +262,27 @@
     return dot(jnp.concatenate([high, low], axis=1), jnp.concatenate([table, table], axis=0))
 
 
-def pack_kernel(count, source_ref, move_ref, a_ref, b_ref, loss_ref, out_ref, loss_out_ref, moves_ref, table_ref):
-    @pl.when(pl.program_id(0) == 0)
+def pack_kernel(count, source_ref, gain_ref, extra_ref, out_ref, extra_out_ref, table_ref):
+    first = pl.program_id(0) == 0
+
+    @pl.when(first)
     def _():
         table_ref[...] = one_hot(source_ref[...], count * count)
-
-    for k in range(moves_ref.shape[0]):
-        moves_ref[k] = one_hot(move_ref[k], 5 * lanes)
 
     def rows_of(ref):
         rows = ref.shape[0] // count
         return jnp.concatenate([ref[pl.ds(k, rows, stride=count), :] for k in range(count)], axis=1)
 
-    terms = out_ref.shape[0]
-    both = jnp.concatenate([rows_of(a_ref), rows_of(b_ref)], axis=0)
-    both = moved(both, table_ref[...]).reshape(2, terms, count, 6 * lanes)
-    for side in range(2):
-        out_ref[:, side] = both[side]
-
-    @pl.when(pl.program_id(0) == 0)
-    def _():
-        loss_out_ref[...] = moved(rows_of(loss_ref), table_ref[...])
+    out_ref[...] = moved(rows_of(gain_ref), table_ref[...]).reshape(out_ref.shape)
+    if extra_ref.shape[1] == count:
+
+        @pl.when(first)
+        def _():
+            extra_out_ref[...] = moved(rows_of(extra_ref), table_ref[...])
+
+    else:
+        for k in range(extra_ref.shape[0]):
+            extra_out_ref[k] = one_hot(extra_ref[k], 5 * lanes)
 
 
 class Cells:
@@ -309,7 +310,8 @@
 
 def first_kernel(
     count, rest, cells, cells_y,
-    density_ref, below_ref, above_ref, kernel_ref, loss_ref, inverse_ref, forward_ref, rows_ref, speed_ref, moves_ref,
+    density_ref, below_ref, above_ref, a_ref, b_ref, loss_ref,
+    inverse_ref, forward_ref, rows_ref, speed_ref, moves_ref,
     field_ref, *refs,
 ):
     up_ref, down_ref = two_rims(refs[:-3])
@@ -338,7 +340,7 @@
         starts = [(x, y * plane // lanes * lanes) for x, y in part]
         values = jnp.concatenate([moved_on[x][:, at : at + 5 * lanes] for x, at in starts], axis=0)
         field_ref[cells.part_rows(k)] = moved_tiles(values, moves_ref[k])
-    collide(field_ref, modes_ref, sum_ref, kernel_ref, loss_ref, inverse_ref, forward_ref, rows_ref, count, rest, 2)
+    collide(field_ref, modes_ref, sum_ref, a_ref, b_ref, loss_ref, inverse_ref, forward_ref, rows_ref, count, rest, 2)
     for x in range(cells_x):
         for k in range(2):
             up_ref[x, k] = field_ref[cells.rows(x, cells_y - 2 + k), 2 * lanes :]
@@ -374,22 +376,22 @@
 
 def inner_kernel(
     count, rest, everything, cells, cells_y,
-    given_ref, kernel_ref, loss_ref, inverse_ref, forward_ref, rows_ref, speed_ref,
+    given_ref, a_ref, b_ref, loss_ref, inverse_ref, forward_ref, rows_ref, speed_ref,
     field_ref, modes_ref, sum_ref,
 ):
     sweep_y(given_ref, None, None, speed_ref, field_ref, everything, cells, cells_y, rest)
-    collide(field_ref, modes_ref, sum_ref, kernel_ref, loss_ref, inverse_ref, forward_ref, rows_ref, count, rest, 4)
+    collide(field_ref, modes_ref, sum_ref, a_ref, b_ref, loss_ref, inverse_ref, forward_ref, rows_ref, count, rest, 4)
 
 
 def outer_kernel(
     count, rest, everything, inner, cells, cells_y,
-    given_ref, inner_ref, kernel_ref, loss_ref, inverse_ref, forward_ref, rows_ref, speed_ref, moves_ref, *refs,
+    given_ref, inner_ref, a_ref, b_ref, loss_ref, inverse_ref, forward_ref, rows_ref, speed_ref, moves_ref, *refs,
 ):
     below_ref, above_ref = two_rims(refs[:-4])
     out_ref, field_ref, modes_ref, sum_ref = refs[-4:]
     plane = count * count
     sweep_y(given_ref, below_ref, above_ref, speed_ref, field_ref, everything, cells, cells_y, rest)
-    collide(field_ref, modes_ref, sum_ref, kernel_ref, loss_ref, inverse_ref, forward_ref, rows_ref, count, rest, 2)
+    collide(field_ref, modes_ref, sum_ref, a_ref, b_ref, loss_ref, inverse_ref, forward_ref, rows_ref, count, rest, 2)
     pieces = {}
     for k in range(2):
         values = [field_ref[cells.part_rows(k)], inner_ref[inner.part_rows(k)]]
@@ -440,41 +442,48 @@
     def cost(cells):
         return pl.CostEstimate(flops=cells.size << 27, bytes_accessed=4 << 20, transcendentals=0)
 
-    below = passed_along(density[-2:, middle:], "gx", 1)
-    above = passed_along(density[:2, :middle], "gx", -1)
     steps = 2 if terms % 2 == 0 else 1
     taken = terms // steps
-    gain_spec = pl.BlockSpec((taken * plane, count), lambda i: (i, 0))
-    packed, packed_loss, move_tables = pl.pallas_call(
-        functools.partial(pack_kernel, count),
-        grid=(steps,),
-        in_specs=[
-            pl.BlockSpec((1, 6 * lanes), lambda i: (0, 0)),
-            pl.BlockSpec((4 // steps, 1, 5 * lanes), lambda i: (i, 0, 0)),
-            gain_spec,
-            gain_spec,
-            pl.BlockSpec((plane, count), lambda i: (0, 0)),
-        ],
-        out_specs=[
-            pl.BlockSpec((taken, 2, count, 6 * lanes), lambda i: (i, 0, 0, 0)),
-            pl.BlockSpec((count, 6 * lanes), lambda i: (0, 0)),
-            pl.BlockSpec((4 // steps, 5 * lanes, 5 * lanes), lambda i: (i, 0, 0)),
-        ],
-        out_shape=(
-            jax.ShapeDtypeStruct((terms, 2, count, 6 * lanes), f32),
-            jax.ShapeDtypeStruct((count, 6 * lanes), f32),
-            jax.ShapeDtypeStruct((4, 5 * lanes, 5 * lanes), bf16),
-        ),
-        scratch_shapes=[pltpu.VMEM((plane, 6 * lanes), bf16)],
-        compiler_params=params(pack_mib),
-        cost_estimate=pl.CostEstimate(flops=4 << 30, bytes_accessed=8 << 20, transcendentals=0),
-        name="pack",
-    )(
-        jnp.asarray(mode_lanes(count)[None]),
+
+    def pack(gains, extra, extra_spec, extra_out_spec, extra_shape):
+        return pl.pallas_call(
+            functools.partial(pack_kernel, count),
+            grid=(steps,),
+            in_specs=[
+                pl.BlockSpec((1, 6 * lanes), lambda i: (0, 0)),
+                pl.BlockSpec((taken * plane, count), lambda i: (i, 0)),
+                extra_spec,
+            ],
+            out_specs=[pl.BlockSpec((taken, count, 6 * lanes), lambda i: (i, 0, 0)), extra_out_spec],
+            out_shape=(jax.ShapeDtypeStruct((terms, count, 6 * lanes), f32), extra_shape),
+            scratch_shapes=[pltpu.VMEM((plane, 6 * lanes), bf16)],
+            compiler_params=params(pack_mib),
+            cost_estimate=pl.CostEstimate(flops=2 << 30, bytes_accessed=4 << 20, transcendentals=0),
+            name="pack",
+        )(
+            jnp.asarray(mode_lanes(count)[None]),
+            pltpu.with_memory_space_constraint(gains.reshape(-1, count), pltpu.HBM),
+            extra,
+        )
+
+    below = passed_along(density[-2:, middle:], "gx", 1)
+    packed_a, packed_loss = pack(
+        gains_a,
+        pltpu.with_memory_space_constraint(loss_rates.reshape(-1, count), pltpu.HBM),
+        pl.BlockSpec((plane, count), lambda i: (0, 0)),
+        pl.BlockSpec((count, 6 * lanes), lambda i: (0, 0)),
+        jax.ShapeDtypeStruct((count, 6 * lanes), f32),
+    )
+    leaving, packed_a, packed_loss, gains_b = lax.optimization_barrier(
+        (density[:2, :middle], packed_a, packed_loss, gains_b)
+    )
+    above = passed_along(leaving, "gx", -1)
+    packed_b, move_tables = pack(
+        gains_b,
         jnp.asarray(moves),
-        gains_a.reshape(-1, count),
-        gains_b.reshape(-1, count),
-        loss_rates.reshape(-1, count),
+        pl.BlockSpec((4 // steps, 1, 5 * lanes), lambda i: (i, 0, 0)),
+        pl.BlockSpec((4 // steps, 5 * lanes, 5 * lanes), lambda i: (i, 0, 0)),
+        jax.ShapeDtypeStruct((4, 5 * lanes, 5 * lanes), bf16),
     )
     rim = (cells_x, 2, count, 3 * lanes)
     mirrored = lax.axis_size("gy") == 2
@@ -486,7 +495,7 @@
         compiler_params=params(first_mib),
         cost_estimate=cost(everything),
         name="first",
-    )(density, below, above, packed, packed_loss, *tables, row_speed, move_tables)
+    )(density, below, above, packed_a, packed_b, packed_loss, *tables, row_speed, move_tables)
     rims = [passed_along(value, "gy", steps) for value, steps in zip(rims, (1, -1))]
     inner_field = pl.pallas_call(
         functools.partial(inner_kernel, count, rest, everything, inner, cells_y),
@@ -495,7 +504,7 @@
         compiler_params=params(second_mib),
         cost_estimate=cost(inner),
         name="inner",
-    )(field, packed, packed_loss, *tables, lane_speed)
+    )(field, packed_a, packed_b, packed_loss, *tables, lane_speed)
     return pl.pallas_call(
         functools.partial(outer_kernel, count, rest, everything, inner, outer, cells_y),
         out_shape=jax.ShapeDtypeStruct(density.shape, f32),
@@ -503,7 +512,7 @@
         compiler_params=params(second_mib),
         cost_estimate=cost(outer),
         name="outer",
-    )(field, inner_field, packed, packed_loss, *tables, lane_speed, move_tables, *rims)
+    )(field, inner_field, packed_a, packed_b, packed_loss, *tables, lane_speed, move_tables, *rims)
 
 
 def solution(mesh):

time: 45.1 us -> 48.9 us (1.084)
  waiting for transfers between devices: 1.4 us -> 6.91 us
  local copies, waits for them, and re-layouts: 6.91 us -> 1.92 us
  Pallas kernels: 29.3 us -> 32.7 us
    ppermute x3, waiting for transfers between devices: 1.4 us -> 6.91 us  [passed_along(): return lax.ppermute(value, axis, pairs)]
    unnamed x22 -> x16, local copies, waits for them, and re-layouts: 5.7 us -> 0.72 us
    pallas_call x1 -> x2, Pallas kernels: 4.16 us -> 7.46 us  [pack(): pl.pallas_call(functools.partial(pack_kernel, count), grid=(steps,), in_s...]
  transfers between devices with their start and end apart: 3 -> 3, of which waited for: 2 -> 3; matrix products, arithmetic and copies ran while one was open for 0% -> 0% of each run, Pallas kernels for 19% -> 18%
where the time goes in v5:
time: 48.9 us; the launch traced here: 48.7 us
  Pallas kernels  32.7 us (67%)
  starting transfers between devices  7.08 us (14%)
  waiting for transfers between devices  6.91 us (14%)
  local copies, waits for them, and re-layouts  1.92 us (4%)
    pallas_call x1, Pallas kernels, body(): pl.pallas_call(functools.partial(first_kernel, count, rest, everything, c...  11.7 us
    pallas_call x1, Pallas kernels, body(): pl.pallas_call(functools.partial(outer_kernel, count, rest, everything, i...  9.21 us
    pallas_call x2, Pallas kernels, pack(): pl.pallas_call(functools.partial(pack_kernel, count), grid=(steps,), in_s...  7.46 us
    ppermute x3, starting transfers between devices, passed_along(): return lax.ppermute(value, axis, pairs)  7.08 us
    ppermute x3, waiting for transfers between devices, passed_along(): return lax.ppermute(value, axis, pairs)  6.91 us
    pallas_call x1, Pallas kernels, body(): pl.pallas_call(functools.partial(inner_kernel, count, rest, everything, i...  4.34 us
    slice x1, local copies, waits for them, and re-layouts, body(): density[:2, :middle]  1.21 us
  transfers between devices with their start and end apart: 3, of which 3 were waited for; matrix products, arithmetic and copies ran while one was open for 0% of the time, Pallas kernels for 18%

profile of v5, /device:TPU:0, one launch (start us, length us, event | category | flops | bytes accessed | tf_op | source)
XLA Modules:
  0.0 48.7 jit_solution(6806456948195093835)
XLA Ops:
  0.0 1.2 %fusion = (f32[2,12,3456]{2,1,0:T(8,128)S(1)}, f32[2,12,3456]{2,1,0:T(8,128)S(1)}) fusion(f32[2,24,3456]{2,1,0:T(8,128)} %density_ref.1), kind=kLoop, calls=%fused_computation | loop fusion | bytes 1327104 | tf_op jit(solution)/shard_map/slice | solution.py:478
  1.2 0.0 copy-start.7
  1.2 0.7 %copy-done.7 = s32[1,768]{1,0:T(1,128)S(1)} copy-done((s32[1,768]{1,0:T(1,128)S(1)}, s32[1,768]{1,0:T(1,128)}, u32[]{:S(2)}) %copy-start.7) | copy-done | bytes 3096
  1.9 0.0 copy-start.6
  1.9 3.1 %pack.2 = (f32[8,24,768]{2,1,0:T(8,128)S(1)}, f32[24,768]{1,0:T(8,128)S(1)}) custom-call(s32[1,768]{1,0:T(1,128)S(1)} %copy-done.7, f32[4608,24]{1,0:T(8,128)} %bitcast.3, f32[576,24]{1,0:T(8,128)} %bitcast.5), custom_call_target="tpu_custom_call" | custom-call | flops 2147483648 | bytes 4194304 | tf_op jit(solution)/shard_map/pack/pallas_call | solution.py:449
  5.1 5.5 %collective-permute-start.1 = (f32[2,12,3456]{2,1,0:T(8,128)S(1)}, f32[2,12,3456]{2,1,0:T(8,128)S(1)}, u32[]{:S(2)}, u32[]{:S(2)}) collective-permute-start(f32[2,12,3456]{2,1,0:T(8,128)S(1)} %get-tuple-element.17), channel_id=1, source_target_pairs={{0,30},{2,0},{4,2},{6,4},{8,6},{10,8},{12,10},{14,12},{16,14},{18,... | collective-permute-start | bytes 995336 | tf_op jit(solution)/shard_map/ppermute | solution.py:24
  10.6 0.0 collective-permute-start
  10.6 0.0 copy-done.6
  10.6 0.0 copy-start
  10.6 0.0 copy-start.1
  10.6 0.0 copy-start.2
  10.6 0.0 copy-start.3
  10.6 0.0 copy-start.4
  10.6 4.3 %pack.3 = (f32[8,24,768]{2,1,0:T(8,128)S(1)}, bf16[4,640,640]{2,1,0:T(8,128)(2,1)S(1)}) custom-call(s32[1,768]{1,0:T(1,128)S(1)} %copy-done.7, f32[4608,24]{1,0:T(8,128)} %bitcast.4, s32[4,1,640]{2,1,0:T(1,128)S(1)} %copy-done.6), custom_call_target="tpu_custom_call" | custom-call | flops 2147483648 | bytes 4194304 | tf_op jit(solution)/shard_map/pack/pallas_call | solution.py:449
  14.9 1.5 %collective-permute-done.1.above_ref = f32[2,12,3456]{2,1,0:T(8,128)S(1)} collective-permute-done((f32[2,12,3456]{2,1,0:T(8,128)S(1)}, f32[2,12,3456]{2,1,0:T(8,128)S(1)}, u32[]{:S(2)}, u32[]{:S(2)}) %collective-permute-start.1) | collective-permute-done | bytes 331808 | tf_op jit(solution)/shard_map/ppermute | solution.py:24
  16.4 4.6 %collective-permute-done.below_ref = f32[2,12,3456]{2,1,0:T(8,128)S(1)} collective-permute-done((f32[2,12,3456]{2,1,0:T(8,128)S(1)}, f32[2,12,3456]{2,1,0:T(8,128)S(1)}, u32[]{:S(2)}, u32[]{:S(2)}) %collective-permute-start) | collective-permute-done | bytes 331808 | tf_op jit(solution)/shard_map/ppermute | solution.py:24
  21.0 0.0 copy-done
  21.0 0.0 copy-done.1
  21.0 0.0 copy-done.2
  21.0 0.0 copy-done.3
  21.0 0.0 copy-done.4
  21.0 0.0 copy-start.5
  21.0 11.7 %first.1 = (f32[288,640]{1,0:T(8,128)S(1)}, f32[2,2,2,24,384]{4,3,2,1,0:T(8,128)S(1)}) custom-call(f32[2,24,3456]{2,1,0:T(8,128)S(1)} %copy-done, f32[2,12,3456]{2,1,0:T(8,128)S(1)} %collective-permute-done.below_ref, f32[2,12,3456]{2,1,0:T(8,128)S(1)} %collective-permute-done.1.above_ref, f32[8,24,768]{2,1,0:T(8,128)S(1)} %get-tuple-element.18.a_ref, ...), custom_call_target="tpu_custom_call" | custom-call | flops 38654705664 | bytes 4194304 | tf_op jit(solution)/shard_map/first/pallas_call | solution.py:491
  32.7 1.6 %collective-permute-start.2 = (f32[2,2,2,24,384]{4,3,2,1,0:T(8,128)S(1)}, f32[2,2,2,24,384]{4,3,2,1,0:T(8,128)S(1)}, u32[]{:S(2)}, u32[]{:S(2)}) collective-permute-start(f32[2,2,2,24,384]{4,3,2,1,0:T(8,128)S(1)} %get-tuple-element.24), channel_id=1, source_target_pairs={{0,1},{1,0},{2,3},{3,2},{4,5},{5,4},{6,7},{7,6},{8,9},{9,8},{10,11... | collective-permute-start | bytes 884744 | tf_op jit(solution)/shard_map/ppermute | solution.py:24
  34.3 0.0 copy-done.5
  34.3 4.3 %inner.1.inner_ref = f32[96,640]{1,0:T(8,128)S(1)} custom-call(f32[288,640]{1,0:T(8,128)S(1)} %get-tuple-element.23.given_ref, f32[8,24,768]{2,1,0:T(8,128)S(1)} %get-tuple-element.18.a_ref, f32[8,24,768]{2,1,0:T(8,128)S(1)} %get-tuple-element.20.b_ref, f32[24,768]{1,0:T(8,128)S(1)} %get-tuple-element.21.loss_ref, bf16[4,512,256]{2,1,0:T(8,128)(2,1)S(1)} %copy-done.2, ...), custom_call_target="tpu_custom_call" | custom-call | flops 12884901888 | bytes 4194304 | tf_op jit(solution)/shard_map/inner/pallas_call | solution.py:500
  38.6 0.9 %collective-permute-done.2.refs_0_ = f32[2,2,2,24,384]{4,3,2,1,0:T(8,128)S(1)} collective-permute-done((f32[2,2,2,24,384]{4,3,2,1,0:T(8,128)S(1)}, f32[2,2,2,24,384]{4,3,2,1,0:T(8,128)S(1)}, u32[]{:S(2)}, u32[]{:S(2)}) %collective-permute-start.2) | collective-permute-done | bytes 294944 | tf_op jit(solution)/shard_map/ppermute | solution.py:24
  39.5 9.2 %outer.1 = f32[2,24,3456]{2,1,0:T(8,128)} custom-call(f32[288,640]{1,0:T(8,128)S(1)} %get-tuple-element.23.given_ref, f32[96,640]{1,0:T(8,128)S(1)} %inner.1.inner_ref, f32[8,24,768]{2,1,0:T(8,128)S(1)} %get-tuple-element.18.a_ref, f32[8,24,768]{2,1,0:T(8,128)S(1)} %get-tuple-element.20.b_ref, f32[24,768]{1,0:T(8,128)S(1)} %get-tuple-element.21.loss_ref, ...), custom_call_target="tpu_custom_call" | custom-call | flops 25769803776 | bytes 4194304 | tf_op jit(solution)/shard_map/outer/pallas_call | solution.py:508
Async XLA Ops:
  1.2 0.7 %copy-start.7 = (s32[1,768]{1,0:T(1,128)S(1)}, s32[1,768]{1,0:T(1,128)}, u32[]{:S(2)}) copy-start(s32[1,768]{1,0:T(1,128)} %constant.19.clone.source_ref) | copy-start | bytes 9220
  1.9 8.7 %copy-start.6 = (s32[4,1,640]{2,1,0:T(1,128)S(1)}, s32[4,1,640]{2,1,0:T(1,128)}, u32[]{:S(2)}) copy-start(s32[4,1,640]{2,1,0:T(1,128)} %constant.20.clone.extra_ref) | copy-start | bytes 30724
  5.1 11.3 %collective-permute-start.1 = (f32[2,12,3456]{2,1,0:T(8,128)S(1)}, f32[2,12,3456]{2,1,0:T(8,128)S(1)}, u32[]{:S(2)}, u32[]{:S(2)}) collective-permute-start(f32[2,12,3456]{2,1,0:T(8,128)S(1)} %get-tuple-element.17), channel_id=1, source_target_pairs={{0,30},{2,0},{4,2},{6,4},{8,6},{10,8},{12,10},{14,12},{16,14},{18,... | collective-permute-start | bytes 995336 | tf_op jit(solution)/shard_map/ppermute | solution.py:24
  10.6 10.4 %collective-permute-start = (f32[2,12,3456]{2,1,0:T(8,128)S(1)}, f32[2,12,3456]{2,1,0:T(8,128)S(1)}, u32[]{:S(2)}, u32[]{:S(2)}) collective-permute-start(f32[2,12,3456]{2,1,0:T(8,128)S(1)} %get-tuple-element.26), channel_id=1, source_target_pairs={{0,2},{2,4},{4,6},{6,8},{8,10},{10,12},{12,14},{14,16},{16,18},{18... | collective-permute-start | bytes 995336 | tf_op jit(solution)/shard_map/ppermute | solution.py:24
  10.6 10.4 %copy-start = (f32[2,24,3456]{2,1,0:T(8,128)S(1)}, f32[2,24,3456]{2,1,0:T(8,128)}, u32[]{:S(2)}) copy-start(f32[2,24,3456]{2,1,0:T(8,128)} %density_ref.1) | copy-start | bytes 1990660
  10.6 10.4 %copy-start.1 = (bf16[4,640,256]{2,1,0:T(8,128)(2,1)S(1)}, bf16[4,640,256]{2,1,0:T(8,128)(2,1)}, u32[]{:S(2)}) copy-start(bf16[4,640,256]{2,1,0:T(8,128)(2,1)} %constant.17.clone.forward_ref) | copy-start | bytes 3932164
  10.6 10.4 %copy-start.2 = (bf16[4,512,256]{2,1,0:T(8,128)(2,1)S(1)}, bf16[4,512,256]{2,1,0:T(8,128)(2,1)}, u32[]{:S(2)}) copy-start(bf16[4,512,256]{2,1,0:T(8,128)(2,1)} %constant.16.clone.inverse_ref) | copy-start | bytes 3145732
  10.6 10.4 %copy-start.3 = (bf16[2,192,192]{2,1,0:T(8,128)(2,1)S(1)}, bf16[2,192,192]{2,1,0:T(8,128)(2,1)}, u32[]{:S(2)}) copy-start(bf16[2,192,192]{2,1,0:T(8,128)(2,1)} %constant.18.clone.rows_ref) | copy-start | bytes 442372
  10.6 10.4 %copy-start.4 = (f32[24,3]{1,0:T(8,128)S(1)}, f32[24,3]{1,0:T(8,128)}, u32[]{:S(2)}) copy-start(f32[24,3]{1,0:T(8,128)} %constant.15.clone.speed_ref) | copy-start | bytes 868
  21.0 13.3 %copy-start.5 = (f32[3,640]{1,0:T(4,128)S(1)}, f32[3,640]{1,0:T(4,128)}, u32[]{:S(2)}) copy-start(f32[3,640]{1,0:T(4,128)} %constant.14.clone.speed_ref) | copy-start | bytes 23044
  32.7 6.8 %collective-permute-start.2 = (f32[2,2,2,24,384]{4,3,2,1,0:T(8,128)S(1)}, f32[2,2,2,24,384]{4,3,2,1,0:T(8,128)S(1)}, u32[]{:S(2)}, u32[]{:S(2)}) collective-permute-start(f32[2,2,2,24,384]{4,3,2,1,0:T(8,128)S(1)} %get-tuple-element.24), channel_id=1, source_target_pairs={{0,1},{1,0},{2,3},{3,2},{4,5},{5,4},{6,7},{7,6},{8,9},{9,8},{10,11... | collective-permute-start | bytes 884744 | tf_op jit(solution)/shard_map/ppermute | solution.py:24

commit v6 on v3

--- a/solution.py
+++ b/solution.py
@@ -304,7 +304,11 @@
 
 
 def two_rims(refs):
-    return (refs[0].at[0], refs[0].at[1]) if len(refs) == 1 else refs
+    return (refs[0], refs[0]) if len(refs) == 1 else refs
+
+
+def backward_lanes(rest):
+    return (lane_index() // (2 * rest)) % 2 == 1
 
 
 def first_kernel(
@@ -341,15 +345,24 @@
     collide(field_ref, modes_ref, sum_ref, kernel_ref, loss_ref, inverse_ref, forward_ref, rows_ref, count, rest, 2)
     for x in range(cells_x):
         for k in range(2):
-            up_ref[x, k] = field_ref[cells.rows(x, cells_y - 2 + k), 2 * lanes :]
-            down_ref[x, k, :, : 2 * lanes] = field_ref[cells.rows(x, k), : 2 * lanes]
-            down_ref[x, k, :, 2 * lanes :] = field_ref[cells.rows(x, k), 4 * lanes :]
+            up, down = cells.rows(x, cells_y - 2 + k), cells.rows(x, k)
+            down_ref[x, k, :, : 2 * lanes] = field_ref[down, : 2 * lanes]
+            if up_ref is down_ref:
+                up_ref[x, k, :, 2 * lanes : 4 * lanes] = field_ref[up, 2 * lanes : 4 * lanes]
+                up_ref[x, k, :, 4 * lanes :] = jnp.where(
+                    backward_lanes(rest), field_ref[up, 4 * lanes :], field_ref[down, 4 * lanes :]
+                )
+            else:
+                up_ref[x, k] = field_ref[up, 2 * lanes :]
+                down_ref[x, k, :, 2 * lanes :] = field_ref[down, 4 * lanes :]
 
 
 def sweep_y(given_ref, below_ref, above_ref, speed_ref, field_ref, everything, cells, cells_y, rest):
-    backward_last = (lane_index() // (2 * rest)) % 2 == 1
+    backward_last = backward_lanes(rest)
 
     def cell(x, y, part):
+        if below_ref is above_ref and not 0 <= y < cells_y:
+            return below_ref[x, y % cells_y % (cells_y - 2), :, part * lanes : (part + 1) * lanes]
         if y < 0:
             return below_ref[x, y + 2, :, (part - 2) * lanes : (part - 1) * lanes]
         if y >= cells_y:
@@ -478,7 +491,7 @@
     )
     rim = (cells_x, 2, count, 3 * lanes)
     mirrored = lax.axis_size("gy") == 2
-    rim_shapes = [jax.ShapeDtypeStruct((2, *rim), f32)] if mirrored else [jax.ShapeDtypeStruct(rim, f32)] * 2
+    rim_shapes = [jax.ShapeDtypeStruct((*rim[:3], 5 * lanes), f32)] if mirrored else [jax.ShapeDtypeStruct(rim, f32)] * 2
     field, *rims = pl.pallas_call(
         functools.partial(first_kernel, count, rest, everything, cells_y),
         out_shape=(jax.ShapeDtypeStruct((everything.size, 5 * lanes), f32), *rim_shapes),

time: 45.1 us -> 44.6 us (0.989)
  waiting for transfers between devices: 1.4 us -> 0.87 us
    ppermute x3, waiting for transfers between devices: 1.4 us -> 0.87 us  [passed_along(): return lax.ppermute(value, axis, pairs)]
where the time goes in v6:
time: 44.6 us; the launch traced here: 44.3 us
  Pallas kernels  29.3 us (66%)
  starting transfers between devices  7.08 us (16%)
  local copies, waits for them, and re-layouts  6.91 us (15%)
  waiting for transfers between devices  0.87 us (2%)
    pallas_call x1, Pallas kernels, body(): pl.pallas_call(functools.partial(first_kernel, count, rest, everything, c...  11.6 us
    pallas_call x1, Pallas kernels, body(): pl.pallas_call(functools.partial(outer_kernel, count, rest, everything, i...  9.19 us
    ppermute x3, starting transfers between devices, passed_along(): return lax.ppermute(value, axis, pairs)  7.08 us
    unnamed x22, local copies, waits for them, and re-layouts  5.7 us
    pallas_call x1, Pallas kernels, body(): pl.pallas_call(functools.partial(inner_kernel, count, rest, everything, i...  4.34 us
    pallas_call x1, Pallas kernels, body(): pl.pallas_call(functools.partial(pack_kernel, count), grid=(steps,), in_s...  4.16 us
    slice x1, local copies, waits for them, and re-layouts, body(): above = passed_along(density[:2, :middle], 'gx', -1)  1.21 us
  transfers between devices with their start and end apart: 3, of which 2 were waited for; matrix products, arithmetic and copies ran while one was open for 0% of the time, Pallas kernels for 19%

profile of v6, /device:TPU:0, one launch (start us, length us, event | category | flops | bytes accessed | tf_op | source)
XLA Modules:
  0.0 44.3 jit_solution(12207976476075369746)
XLA Ops:
  0.0 1.2 %fusion = (f32[2,12,3456]{2,1,0:T(8,128)S(1)}, f32[2,12,3456]{2,1,0:T(8,128)S(1)}) fusion(f32[2,24,3456]{2,1,0:T(8,128)} %density_ref.1), kind=kLoop, calls=%fused_computation | loop fusion | bytes 1327104 | tf_op jit(solution)/shard_map/slice | solution.py:457
  1.2 5.5 %collective-permute-start.1 = (f32[2,12,3456]{2,1,0:T(8,128)S(1)}, f32[2,12,3456]{2,1,0:T(8,128)S(1)}, u32[]{:S(2)}, u32[]{:S(2)}) collective-permute-start(f32[2,12,3456]{2,1,0:T(8,128)S(1)} %get-tuple-element.15), channel_id=1, source_target_pairs={{0,30},{2,0},{4,2},{6,4},{8,6},{10,8},{12,10},{14,12},{16,14},{18,... | collective-permute-start | bytes 995336 | tf_op jit(solution)/shard_map/ppermute | solution.py:23
  6.7 0.0 collective-permute-start
  6.7 0.0 copy-start.1
  6.7 1.7 %copy-done.1 = f32[8,24,24,24]{3,2,1,0:T(8,128)S(1)} copy-done((f32[8,24,24,24]{3,2,1,0:T(8,128)S(1)}, f32[8,24,24,24]{3,2,1,0:T(8,128)}, u32[]{:S(2)}) %copy-start.1) | copy-done | bytes 442392
  8.4 0.0 copy-start.2
  8.4 1.7 %copy-done.2 = f32[8,24,24,24]{3,2,1,0:T(8,128)S(1)} copy-done((f32[8,24,24,24]{3,2,1,0:T(8,128)S(1)}, f32[8,24,24,24]{3,2,1,0:T(8,128)}, u32[]{:S(2)}) %copy-start.2) | copy-done | bytes 442392
  10.0 0.0 copy-start.3
  10.0 1.0 %copy-done.3 = f32[24,24,24]{2,1,0:T(8,128)S(1)} copy-done((f32[24,24,24]{2,1,0:T(8,128)S(1)}, f32[24,24,24]{2,1,0:T(8,128)}, u32[]{:S(2)}) %copy-start.3) | copy-done | bytes 55320
  11.0 0.0 copy-start.9
  11.0 0.7 %copy-done.9 = s32[4,1,640]{2,1,0:T(1,128)S(1)} copy-done((s32[4,1,640]{2,1,0:T(1,128)S(1)}, s32[4,1,640]{2,1,0:T(1,128)}, u32[]{:S(2)}) %copy-start.9) | copy-done | bytes 10264
  11.7 0.0 copy-start.10
  11.7 0.7 %copy-done.10 = s32[1,768]{1,0:T(1,128)S(1)} copy-done((s32[1,768]{1,0:T(1,128)S(1)}, s32[1,768]{1,0:T(1,128)}, u32[]{:S(2)}) %copy-start.10) | copy-done | bytes 3096
  12.4 0.0 copy-start
  12.4 0.0 copy-start.4
  12.4 0.0 copy-start.5
  12.4 0.0 copy-start.7
  12.4 4.2 %pack.1 = (f32[8,2,24,768]{3,2,1,0:T(8,128)S(1)}, f32[24,768]{1,0:T(8,128)S(1)}, bf16[4,640,640]{2,1,0:T(8,128)(2,1)S(1)}) custom-call(s32[1,768]{1,0:T(1,128)S(1)} %copy-done.10, s32[4,1,640]{2,1,0:T(1,128)S(1)} %copy-done.9, f32[4608,24]{1,0:T(8,128)S(1)} %bitcast.3, f32[4608,24]{1,0:T(8,128)S(1)} %bitcast.4, f32[576,24]{1,0:T(8,128)S(1)} %bitcast.5), custom_call_target="tpu_custom_call" | custom-call | flops 4294967296 | bytes 8388608 | tf_op jit(solution)/shard_map/pack/pallas_call | solution.py:461
  16.6 0.0 collective-permute-done.1.above_ref
  16.6 0.5 %collective-permute-done.below_ref = f32[2,12,3456]{2,1,0:T(8,128)S(1)} collective-permute-done((f32[2,12,3456]{2,1,0:T(8,128)S(1)}, f32[2,12,3456]{2,1,0:T(8,128)S(1)}, u32[]{:S(2)}, u32[]{:S(2)}) %collective-permute-start) | collective-permute-done | bytes 331808 | tf_op jit(solution)/shard_map/ppermute | solution.py:23
  17.1 0.0 copy-done
  17.1 0.0 copy-done.4
  17.1 0.0 copy-done.5
  17.1 0.0 copy-done.6
  17.2 0.0 copy-done.7
  17.2 0.0 copy-start.8
  17.2 11.6 %first.1 = (f32[288,640]{1,0:T(8,128)S(1)}, f32[2,2,24,640]{3,2,1,0:T(8,128)S(1)}) custom-call(f32[2,24,3456]{2,1,0:T(8,128)S(1)} %copy-done, f32[2,12,3456]{2,1,0:T(8,128)S(1)} %collective-permute-done.below_ref, f32[2,12,3456]{2,1,0:T(8,128)S(1)} %collective-permute-done.1.above_ref, f32[8,2,24,768]{3,2,1,0:T(8,128)S(1)} %get-tuple-element.10.kernel_ref, ...), custom_call_target="tpu_custom_call" | custom-call | flops 38654705664 | bytes 4194304 | tf_op jit(solution)/shard_map/first/pallas_call | solution.py:495
  28.8 1.6 %collective-permute-start.2 = (f32[2,2,24,640]{3,2,1,0:T(8,128)S(1)}, f32[2,2,24,640]{3,2,1,0:T(8,128)S(1)}, u32[]{:S(2)}, u32[]{:S(2)}) collective-permute-start(f32[2,2,24,640]{3,2,1,0:T(8,128)S(1)} %get-tuple-element.14), channel_id=1, source_target_pairs={{0,1},{1,0},{2,3},{3,2},{4,5},{5,4},{6,7},{7,6},{8,9},{9,8},{10,11... | collective-permute-start | bytes 737288 | tf_op jit(solution)/shard_map/ppermute | solution.py:23
  30.4 0.0 copy-done.8
  30.4 4.3 %inner.1.inner_ref = f32[96,640]{1,0:T(8,128)S(1)} custom-call(f32[288,640]{1,0:T(8,128)S(1)} %get-tuple-element.13.given_ref, f32[8,2,24,768]{3,2,1,0:T(8,128)S(1)} %get-tuple-element.10.kernel_ref, f32[24,768]{1,0:T(8,128)S(1)} %get-tuple-element.11.loss_ref, bf16[4,512,256]{2,1,0:T(8,128)(2,1)S(1)} %copy-done.5, bf16[4,640,256]{2,1,0:T(8,128)(2,1)S(1)} %copy-done.4, ...), custom_call_target="tpu_custom_call" | custom-call | flops 12884901888 | bytes 4194304 | tf_op jit(solution)/shard_map/inner/pallas_call | solution.py:504
  34.7 0.3 collective-permute-done.2.refs_0_
  35.1 9.2 %outer.1 = f32[2,24,3456]{2,1,0:T(8,128)} custom-call(f32[288,640]{1,0:T(8,128)S(1)} %get-tuple-element.13.given_ref, f32[96,640]{1,0:T(8,128)S(1)} %inner.1.inner_ref, f32[8,2,24,768]{3,2,1,0:T(8,128)S(1)} %get-tuple-element.10.kernel_ref, f32[24,768]{1,0:T(8,128)S(1)} %get-tuple-element.11.loss_ref, bf16[4,512,256]{2,1,0:T(8,128)(2,1)S(1)} %copy-done.5, ...), custom_call_target="tpu_custom_call" | custom-call | flops 25769803776 | bytes 4194304 | tf_op jit(solution)/shard_map/outer/pallas_call | solution.py:512
  (1 shorter events, 0.0 us)
Async XLA Ops:
  1.2 15.4 %collective-permute-start.1 = (f32[2,12,3456]{2,1,0:T(8,128)S(1)}, f32[2,12,3456]{2,1,0:T(8,128)S(1)}, u32[]{:S(2)}, u32[]{:S(2)}) collective-permute-start(f32[2,12,3456]{2,1,0:T(8,128)S(1)} %get-tuple-element.15), channel_id=1, source_target_pairs={{0,30},{2,0},{4,2},{6,4},{8,6},{10,8},{12,10},{14,12},{16,14},{18,... | collective-permute-start | bytes 995336 | tf_op jit(solution)/shard_map/ppermute | solution.py:23
  6.7 10.4 %collective-permute-start = (f32[2,12,3456]{2,1,0:T(8,128)S(1)}, f32[2,12,3456]{2,1,0:T(8,128)S(1)}, u32[]{:S(2)}, u32[]{:S(2)}) collective-permute-start(f32[2,12,3456]{2,1,0:T(8,128)S(1)} %get-tuple-element.16), channel_id=1, source_target_pairs={{0,2},{2,4},{4,6},{6,8},{8,10},{10,12},{12,14},{14,16},{16,18},{18... | collective-permute-start | bytes 995336 | tf_op jit(solution)/shard_map/ppermute | solution.py:23
  6.7 1.7 %copy-start.1 = (f32[8,24,24,24]{3,2,1,0:T(8,128)S(1)}, f32[8,24,24,24]{3,2,1,0:T(8,128)}, u32[]{:S(2)}) copy-start(f32[8,24,24,24]{3,2,1,0:T(8,128)} %param.12) | copy-start | bytes 1327108
  8.4 1.7 %copy-start.2 = (f32[8,24,24,24]{3,2,1,0:T(8,128)S(1)}, f32[8,24,24,24]{3,2,1,0:T(8,128)}, u32[]{:S(2)}) copy-start(f32[8,24,24,24]{3,2,1,0:T(8,128)} %param.13) | copy-start | bytes 1327108
  10.0 1.0 %copy-start.3 = (f32[24,24,24]{2,1,0:T(8,128)S(1)}, f32[24,24,24]{2,1,0:T(8,128)}, u32[]{:S(2)}) copy-start(f32[24,24,24]{2,1,0:T(8,128)} %param.14) | copy-start | bytes 165892
  11.0 0.7 %copy-start.9 = (s32[4,1,640]{2,1,0:T(1,128)S(1)}, s32[4,1,640]{2,1,0:T(1,128)}, u32[]{:S(2)}) copy-start(s32[4,1,640]{2,1,0:T(1,128)} %constant.20.clone.move_ref) | copy-start | bytes 30724
  11.7 0.7 %copy-start.10 = (s32[1,768]{1,0:T(1,128)S(1)}, s32[1,768]{1,0:T(1,128)}, u32[]{:S(2)}) copy-start(s32[1,768]{1,0:T(1,128)} %constant.19.clone.source_ref) | copy-start | bytes 9220
  12.4 4.7 %copy-start = (f32[2,24,3456]{2,1,0:T(8,128)S(1)}, f32[2,24,3456]{2,1,0:T(8,128)}, u32[]{:S(2)}) copy-start(f32[2,24,3456]{2,1,0:T(8,128)} %density_ref.1) | copy-start | bytes 1990660
  12.4 4.7 %copy-start.4 = (bf16[4,640,256]{2,1,0:T(8,128)(2,1)S(1)}, bf16[4,640,256]{2,1,0:T(8,128)(2,1)}, u32[]{:S(2)}) copy-start(bf16[4,640,256]{2,1,0:T(8,128)(2,1)} %constant.17.clone.forward_ref) | copy-start | bytes 3932164
  12.4 4.7 %copy-start.5 = (bf16[4,512,256]{2,1,0:T(8,128)(2,1)S(1)}, bf16[4,512,256]{2,1,0:T(8,128)(2,1)}, u32[]{:S(2)}) copy-start(bf16[4,512,256]{2,1,0:T(8,128)(2,1)} %constant.16.clone.inverse_ref) | copy-start | bytes 3145732
  12.4 4.7 %copy-start.6 = (bf16[2,192,192]{2,1,0:T(8,128)(2,1)S(1)}, bf16[2,192,192]{2,1,0:T(8,128)(2,1)}, u32[]{:S(2)}) copy-start(bf16[2,192,192]{2,1,0:T(8,128)(2,1)} %constant.18.clone.rows_ref) | copy-start | bytes 442372
  12.4 4.8 %copy-start.7 = (f32[24,3]{1,0:T(8,128)S(1)}, f32[24,3]{1,0:T(8,128)}, u32[]{:S(2)}) copy-start(f32[24,3]{1,0:T(8,128)} %constant.15.clone.speed_ref) | copy-start | bytes 868
  17.2 13.2 %copy-start.8 = (f32[3,640]{1,0:T(4,128)S(1)}, f32[3,640]{1,0:T(4,128)}, u32[]{:S(2)}) copy-start(f32[3,640]{1,0:T(4,128)} %constant.14.clone.speed_ref) | copy-start | bytes 23044
  28.8 6.3 %collective-permute-start.2 = (f32[2,2,24,640]{3,2,1,0:T(8,128)S(1)}, f32[2,2,24,640]{3,2,1,0:T(8,128)S(1)}, u32[]{:S(2)}, u32[]{:S(2)}) collective-permute-start(f32[2,2,24,640]{3,2,1,0:T(8,128)S(1)} %get-tuple-element.14), channel_id=1, source_target_pairs={{0,1},{1,0},{2,3},{3,2},{4,5},{5,4},{6,7},{7,6},{8,9},{9,8},{10,11... | collective-permute-start | bytes 737288 | tf_op jit(solution)/shard_map/ppermute | solution.py:23
